TPU v7x, 512 devices: a whole 4x4x16 slice. The times are simulated.
512 devices in a mesh: cls: 32 (over z_hi, y, x), slab: 16 (over z_lo, core).
Axes of the slice: x: 4, y: 4, z: 16 (z_hi: 2, z_lo: 8; z = z_hi * 8 + z_lo), core: 2. Of those that a mesh axis runs over, the one named last changes fastest.
Arguments:
- q_init: bfloat16 [32, 256, 64, 128], P('cls', 'slab'), may hold values from 0.5 to 2
- q_back: bfloat16 [32, 4, 256, 64, 128], P('cls', None, 'slab'), may hold values from 0.5 to 2
- fields: float32 [2, 256, 64, 128], P(None, 'slab'), may hold values from -4 to 4
- lengths: int32 [32], replicated, may hold values from 16 to 63
- steps_count: int32 [32], replicated, may hold values from 64 to 127
- block_types: int32 [32, 4], replicated, may hold values from 0 to 1
Outputs:
- fields_new: float32 [2, 256, 64, 128], P(None, 'slab')
- q_final: bfloat16 [32, 256, 64, 128], P('cls', 'slab')
Inputs may be any that keep to these rules, and one draw needn't show every extreme that they name: `steps_count`: steps of each class's whole chain.
All inputs are finite; a program needn't handle non-finite values.
Results may differ from a plain program's by a relative error of at most 0.001.
Values sent between devices are 32-bit elements; how exact they have to be, the bound alone decides.
No kernel may reach another device: no remote copies, remote signals or barrier semaphores. Data moves between devices by JAX's collectives and lax.ppermute only.
A program may use at most 64 MiB of HBM per device.

v0:
```python
import jax
import jax.numpy as jnp
from jax import lax
from jax.sharding import Mesh
from jax.sharding import PartitionSpec as P

CLS = ("cls_0", "cls_1", "cls_2")


flory_chi = 2.0
stiffness = 1.0
mixing = 0.5
diffusion_scale = 0.125


def padded_2(block, sides, width):
    for axis, dim in sides:
        count = lax.axis_size(axis)
        forward = [(i, i + 1) for i in range(count - 1)]
        backward = [(target, source) for source, target in forward]
        low = lax.ppermute(
            lax.slice_in_dim(block, block.shape[dim] - width, None, axis=dim), axis, forward
        )
        high = lax.ppermute(lax.slice_in_dim(block, 0, width, axis=dim), axis, backward)
        block = jnp.concatenate([low, block, high], axis=dim)
    return block


def sent_to_all(x, axis):
    peers = lax.axis_size(axis)
    return lax.all_to_all(jnp.broadcast_to(x[None], (peers, *x.shape)), axis, 0, 0, tiled=True)


def over_copies(x, axis):
    everything = sent_to_all(x, axis)
    return jnp.sum(everything, axis=0)


def split_up(x, dim, peers):
    before, after = (x.shape[:dim], x.shape[dim + 1 :])
    return jnp.moveaxis(x.reshape(*before, peers, -1, *after), dim, 0)


def summed_on_arrival(x, axis, dim):
    peers = lax.axis_size(axis)
    tiles = lax.all_to_all(split_up(x, dim, peers), axis, 0, 0, tiled=True)
    return jnp.sum(tiles, axis=0)


def summed_rows(x, axes, dim):
    far, near = axes
    tiles = split_up(x, dim, lax.axis_size(far))
    nearer = summed_on_arrival(tiles, near, dim + 1)
    arrived = lax.all_to_all(nearer, far, split_axis=0, concat_axis=0, tiled=True)
    return arrived.sum(axis=0)


def filled_up(lines, peers):
    spare = -len(lines) % peers
    return jnp.pad(lines, [(0, spare)] + [(0, 0)] * (lines.ndim - 1))


def joined_along(tiles, dim):
    shape = list(tiles.shape[1:])
    shape[dim] *= tiles.shape[0]
    return jnp.moveaxis(tiles, 0, dim).reshape(shape)


def whole_of(x, axes, dim):
    far, near = axes
    initial = sent_to_all(x, far)
    tiles = jnp.swapaxes(sent_to_all(initial, near), 0, 1)
    return joined_along(tiles.reshape(-1, *x.shape), dim)


def sum_by_parts(x, axes):
    lines = x.reshape(-1, x.shape[-1])
    own = summed_rows(filled_up(lines, lax.axis_size(axes[0]) * lax.axis_size(axes[1])), axes, 0)
    whole = whole_of(own, axes, 0)
    return whole[: len(lines)].reshape(x.shape)


def column(values):
    return values[:, None, None, None]


def stencil_core(extended):
    core = extended[:, 1:-1]
    total = extended[:, 2:] + extended[:, :-2]
    padded = jnp.pad(core, ((0, 0), (0, 0), (1, 1), (1, 1)))
    total = total + padded[:, :, 2:, 1:-1] + padded[:, :, :-2, 1:-1]
    total = total + padded[:, :, 1:-1, 2:] + padded[:, :, 1:-1, :-2]
    return (core, total)


def update_fields(density, old_fields, level):
    total = density[0] + density[1]
    pressure = stiffness * (total - level)
    first = old_fields[0] + mixing * (flory_chi * density[1] + pressure - old_fields[0])
    second = old_fields[1] + mixing * (flory_chi * density[0] + pressure - old_fields[1])
    return jnp.stack([first, second])


def body(q_init, q_back, fields, lengths, steps_count, block_types):
    class_count = q_init.shape[0]
    planes = q_init.shape[1]
    width_x = q_init.shape[2]
    width_y = q_init.shape[3]
    depth = q_back.shape[1]
    cells = lax.axis_size("slab") * planes * width_x * width_y
    first_class = lax.axis_index(CLS) * class_count
    size_all = lengths.astype(jnp.float32) / steps_count.astype(jnp.float32)
    share_all = lengths.astype(jnp.float32) / jnp.sum(lengths).astype(jnp.float32)
    step_size = lax.dynamic_slice_in_dim(size_all, first_class, class_count)
    fraction = lax.dynamic_slice_in_dim(share_all, first_class, class_count)
    types = lax.dynamic_slice_in_dim(block_types, first_class, class_count, 0)
    spread = diffusion_scale * step_size
    products = []
    stacked = jnp.concatenate([q_init.astype(jnp.float32), fields], 0)
    extended = padded_2(stacked, (("slab", 1),), depth)
    forward = extended[:class_count]
    field_ext = extended[class_count:]
    positions = (
        lax.axis_index("slab") * planes - depth + jnp.arange(planes + 2 * depth, dtype=jnp.int32)
    )
    for step in range(depth):
        chosen = jnp.where(column(types[:, step] == 0), field_ext[0][None], field_ext[1][None])
        half = jnp.exp(-0.5 * column(step_size) * chosen)
        weighted = half * forward
        core, total = stencil_core(weighted)
        fresh = half[:, 1:-1] * ((1.0 - 6.0 * column(spread)) * core + column(spread) * total)
        inside_pos = positions[step + 1 : positions.shape[0] - step - 1]
        inside = (inside_pos >= 0) & (inside_pos < cells // (planes * width_x * width_y) * planes)
        forward = jnp.where(inside[None, :, None, None], fresh, 0.0)
        field_ext = field_ext[:, 1:-1]
        offset = depth - step - 1
        middle = forward[:, offset : offset + planes]
        products.append(middle * q_back[:, step].astype(jnp.float32))
    local_part = jnp.sum(products[0], axis=(1, 2, 3))
    partition = over_copies(local_part, "slab") / cells
    weight = fraction * step_size / partition
    density = jnp.zeros((2, planes, width_x, width_y), jnp.float32)
    for step in range(depth):
        select = (jnp.arange(2, dtype=jnp.int32)[None, :] == types[:, step : step + 1]).astype(
            jnp.float32
        )
        factor = weight[:, None] * select
        density = density + jnp.einsum(
            "ct,czxy->tzxy", factor, products[step], precision=lax.Precision.HIGHEST
        )
    whole = sum_by_parts(density, ("cls_0", ("cls_1", "cls_2")))
    level = over_copies(jnp.sum(whole[0] + whole[1]), "slab") / cells
    fields_new = update_fields(whole, fields, level)
    return (fields_new, forward.astype(jnp.bfloat16))


def solution(mesh):
    finer = Mesh(
        mesh.devices.reshape(2, 4, 4, mesh.shape["slab"]), ("cls_0", "cls_1", "cls_2", "slab")
    )
    in_specs = (
        P(CLS, "slab", None, None),
        P(CLS, None, "slab", None, None),
        P(None, "slab", None, None),
        P(),
        P(),
        P(),
    )
    out_specs = (P(None, "slab", None, None), P(CLS, "slab", None, None))
    return jax.shard_map(body, mesh=finer, in_specs=in_specs, out_specs=out_specs, check_vma=False)
```

profile of v0, /device:TPU:1, one launch (start us, length us, event | category | flops | bytes accessed | tf_op | source)
XLA Modules:
  0.0 143.8 jit_solution(7593139853842698010)
XLA Ops:
  0.7 1.1 convert_element_type.87
  1.8 1.1 pad_maximum_fusion.3
  2.9 4.9 %collective-permute-start = (f32[3,4,64,128]{3,2,1,0:T(8,128)S(1)}, f32[3,4,64,128]{3,2,1,0:T(8,128)S(1)}, u32[]{:S(2)}, u32[]{:S(2)}) collective-permute-start(f32[3,4,64,128]{3,2,1,0:T(8,128)S(1)} %get-tuple-element.25), channel_id=1, source_target_pairs={{0,1},{1,2},{2,3},{3,4},{4,5},{5,6},{6,7},{7,8},{8,9},{9,10},{10,1... | collective-permute-start | bytes 1179656 | tf_op jit(solution)/shard_map/ppermute | solution.py:21
  7.8 5.1 %collective-permute-start.1 = (f32[3,4,64,128]{3,2,1,0:T(8,128)S(1)}, f32[3,4,64,128]{3,2,1,0:T(8,128)S(1)}, u32[]{:S(2)}, u32[]{:S(2)}) collective-permute-start(f32[3,4,64,128]{3,2,1,0:T(8,128)S(1)} %get-tuple-element.26), channel_id=1, source_target_pairs={{1,0},{2,1},{3,2},{4,3},{5,4},{6,5},{7,6},{8,7},{9,8},{10,9},{11,1... | collective-permute-start | bytes 1179656 | tf_op jit(solution)/shard_map/ppermute | solution.py:24
  13.1 0.6 reduce_sum.63
  20.6 0.7 fusion.60
  21.4 0.6 fusion.57
  22.7 1.1 fusion.52
  23.9 0.9 fusion.45
  24.8 1.2 broadcast_in_dim.144
  26.0 9.5 %all-to-all-start = ((f32[16,1,1]{2,1,0:T(1,128)}), f32[16,1,1]{2,1,0:T(1,128)S(1)}, u32[]{:S(2)}, u32[]{:S(2)}) async-start(f32[16,1,1]{2,1,0:T(1,128)} %broadcast_in_dim.144), calls=%async_computation | async-start | bytes 16384 | tf_op jit(solution)/shard_map/all_to_all | solution.py:31
  37.3 7.9 %all-to-all-done = f32[16,1,1]{2,1,0:T(1,128)S(1)} async-done(((f32[16,1,1]{2,1,0:T(1,128)}), f32[16,1,1]{2,1,0:T(1,128)S(1)}, u32[]{:S(2)}, u32[]{:S(2)}) %all-to-all-start) | async-done | bytes 96 | tf_op jit(solution)/shard_map/all_to_all | solution.py:31
  45.2 0.6 reduce_sum.65
  46.5 1.2 fusion.49
  47.7 1.2 fusion.47
  49.3 22.6 %all_to_all.32 = f32[16,2,64,128]{3,2,1,0:T(8,128)S(1)} all-to-all(f32[16,2,64,128]{3,2,1,0:T(8,128)S(1)} %add_bitcast_fusion), channel_id=1, replica_groups=mesh['cls_0'=2,'cls_1'=4,'cls_2'=4,'slab'=16] {'cls_1','cls_2'}, dimensions={0} | all-to-all | bytes 2097152 | tf_op jit(solution)/shard_map/all_to_all | solution.py:46
  72.0 18.8 %all_to_all.33 = f32[2,64,128]{2,1,0:T(8,128)S(1)} all-to-all(f32[2,64,128]{2,1,0:T(8,128)S(1)} %reduce_sum.66), channel_id=1, replica_groups=mesh['cls_0'=2,'cls_1'=4,'cls_2'=4,'slab'=16] {'cls_0'}, dimensions={0} | all-to-all | bytes 131072 | tf_op jit(solution)/shard_map/all_to_all | solution.py:54
  90.8 14.1 %all_to_all.34 = f32[2,64,128]{2,1,0:T(8,128)S(1)} all-to-all(f32[2,64,128]{2,1,0:T(8,128)S(1)} %broadcast_in_dim.157), channel_id=1, replica_groups=mesh['cls_0'=2,'cls_1'=4,'cls_2'=4,'slab'=16] {'cls_0'}, dimensions={0} | all-to-all | bytes 131072 | tf_op jit(solution)/shard_map/all_to_all | solution.py:31
  105.0 17.1 %all_to_all.35 = f32[16,2,64,128]{3,2,1,0:T(8,128)S(1)} all-to-all(f32[16,2,64,128]{3,2,1,0:T(8,128)S(1)} %broadcast_in_dim.158), channel_id=1, replica_groups=mesh['cls_0'=2,'cls_1'=4,'cls_2'=4,'slab'=16] {'cls_1','cls_2'}, dimensions={0} | all-to-all | bytes 2097152 | tf_op jit(solution)/shard_map/all_to_all | solution.py:31
  122.1 0.7 fusion.51
  122.8 0.6 broadcast_in_dim.159
  123.5 17.6 %all_to_all.36 = f32[16,1,1]{2,1,0:T(1,128)S(1)} all-to-all(f32[16,1,1]{2,1,0:T(1,128)S(1)} %broadcast_in_dim.159), channel_id=1, replica_groups=mesh['cls_0'=2,'cls_1'=4,'cls_2'=4,'slab'=16] {'slab'}, dimensions={0} | all-to-all | bytes 128 | tf_op jit(solution)/shard_map/all_to_all | solution.py:31
  141.1 0.6 reduce_sum.69
  142.7 1.1 copy.18
  (36 shorter events, 4.2 us)
Async XLA Ops:
  0.6 16.2 %copy-start = (s32[32,4]{0,1:T(4,128)S(1)}, s32[32,4]{0,1:T(4,128)}, u32[]{:S(2)}) copy-start(s32[32,4]{0,1:T(4,128)} %param.11) | copy-start | bytes 1540
  0.6 19.5 %copy-start.1 = (f32[2,16,64,128]{3,2,1,0:T(8,128)S(1)}, f32[2,16,64,128]{3,2,1,0:T(8,128)}, u32[]{:S(2)}) copy-start(f32[2,16,64,128]{3,2,1,0:T(8,128)} %param.8) | copy-start | bytes 3145732
  0.7 12.4 %copy-start.3 = (s32[32]{0:T(128)S(1)}, s32[32]{0:T(128)}, u32[]{:S(2)}) copy-start(s32[32]{0:T(128)} %param.9) | copy-start | bytes 388
  0.7 13.7 %copy-start.4 = (s32[32]{0:T(128)S(1)}, s32[32]{0:T(128)}, u32[]{:S(2)}) copy-start(s32[32]{0:T(128)} %param.10) | copy-start | bytes 388
  2.9 17.3 %collective-permute-start = (f32[3,4,64,128]{3,2,1,0:T(8,128)S(1)}, f32[3,4,64,128]{3,2,1,0:T(8,128)S(1)}, u32[]{:S(2)}, u32[]{:S(2)}) collective-permute-start(f32[3,4,64,128]{3,2,1,0:T(8,128)S(1)} %get-tuple-element.25), channel_id=1, source_target_pairs={{0,1},{1,2},{2,3},{3,4},{4,5},{5,6},{6,7},{7,8},{8,9},{9,10},{10,1... | collective-permute-start | bytes 1179656 | tf_op jit(solution)/shard_map/ppermute | solution.py:21
  7.8 12.4 %collective-permute-start.1 = (f32[3,4,64,128]{3,2,1,0:T(8,128)S(1)}, f32[3,4,64,128]{3,2,1,0:T(8,128)S(1)}, u32[]{:S(2)}, u32[]{:S(2)}) collective-permute-start(f32[3,4,64,128]{3,2,1,0:T(8,128)S(1)} %get-tuple-element.26), channel_id=1, source_target_pairs={{1,0},{2,1},{3,2},{4,3},{5,4},{6,5},{7,6},{8,7},{9,8},{10,9},{11,1... | collective-permute-start | bytes 1179656 | tf_op jit(solution)/shard_map/ppermute | solution.py:24
  22.7 1.2 copy-start.2
  26.0 19.2 %all-to-all-start = ((f32[16,1,1]{2,1,0:T(1,128)}), f32[16,1,1]{2,1,0:T(1,128)S(1)}, u32[]{:S(2)}, u32[]{:S(2)}) async-start(f32[16,1,1]{2,1,0:T(1,128)} %broadcast_in_dim.144), calls=%async_computation | async-start | bytes 16384 | tf_op jit(solution)/shard_map/all_to_all | solution.py:31
where the time goes:
time: 144 us
  blocking collectives  90.2 us (63%)
  starting transfers between devices  19.6 us (14%)
  other arithmetic  12.6 us (9%)
  between operations  8.37 us (6%)
  waiting for transfers between devices  7.9 us (5%)
  local copies, waits for them, and re-layouts  5.13 us (4%)
    all_to_all x3, blocking collectives, sent_to_all(): lax.all_to_all(jnp.broadcast_to(x[None], (peers, *x.shape)), axis, 0, 0,...  48.8 us
    all_to_all x1, blocking collectives, summed_on_arrival(): tiles = lax.all_to_all(split_up(x, dim, peers), axis, 0, 0, tiled=True)  22.6 us
    all_to_all x1, blocking collectives, summed_rows(): lax.all_to_all(nearer, far, split_axis=0, concat_axis=0, tiled=True)  18.8 us
    all_to_all x1, starting transfers between devices, sent_to_all(): lax.all_to_all(jnp.broadcast_to(x[None], (peers, *x.shape)), axis, 0, 0,...  9.53 us
    all_to_all x1, waiting for transfers between devices, sent_to_all(): lax.all_to_all(jnp.broadcast_to(x[None], (peers, *x.shape)), axis, 0, 0,...  7.89 us
    ppermute x1, starting transfers between devices, padded_2(): lax.ppermute(lax.slice_in_dim(block, 0, width, axis=dim), axis, backward)  5.14 us
    ppermute x1, starting transfers between devices, padded_2(): lax.ppermute(lax.slice_in_dim(block, block.shape[dim] - width, None, axis...  4.92 us
  transfers between devices with their start and end apart: 3, of which 1 were waited for; matrix products, arithmetic and copies ran while one was open for 2% of the time, Pallas kernels for 0%

commit v1 on v0

v1 whole, which is shorter than its diff:
```python
import functools

import jax
import jax.numpy as jnp
from jax import lax
from jax.experimental import pallas as pl
from jax.experimental.pallas import tpu as pltpu
from jax.sharding import Mesh
from jax.sharding import PartitionSpec as P

CLS = ("zh", "y", "x")
XY = ("y", "x")
SLAB = "slab"

flory_chi = 2.0
stiffness = 1.0
mixing = 0.5
diffusion_scale = 0.125

VMEM = pl.BlockSpec(memory_space=pltpu.VMEM)
SMEM = pl.BlockSpec(memory_space=pltpu.SMEM)
TOP = 8


def own_class():
    return (lax.axis_index("zh") * 4 + lax.axis_index("y")) * 4 + lax.axis_index("x")


def splat(value, shape=(1, 128)):
    return jnp.full(shape, value, jnp.float32)


def size_of(lengths, counts, cls):
    return splat(lengths[cls].astype(jnp.float32)) / splat(counts[cls].astype(jnp.float32))


def folded(plane):
    return jnp.sum(plane.reshape(-1, 8, plane.shape[-1]), axis=0)


def neighbours(w, slot, p, lane_low, lane_high, nx):
    core = w[slot, p, TOP : TOP + nx, :]
    total = w[slot, p - 1, TOP : TOP + nx, :] + w[slot, p + 1, TOP : TOP + nx, :]
    total = total + w[slot, p, TOP - 1 : TOP + nx - 1, :] + w[slot, p, TOP + 1 : TOP + nx + 1, :]
    ny = core.shape[-1]
    before = jnp.where(lane_low, 0.0, pltpu.roll(core, 1, 1))
    after = jnp.where(lane_high, 0.0, pltpu.roll(core, ny - 1, 1))
    return core, total + before + after


def lane_edges(nx, ny):
    lane = lax.broadcasted_iota(jnp.int32, (nx, ny), 1)
    return lane == 0, lane == ny - 1


def clear_margins(w, nx):
    blank = jnp.zeros(w.shape[:2] + (TOP, w.shape[-1]), jnp.float32)
    w[:, :, 0:TOP, :] = blank
    w[:, :, TOP + nx : TOP + nx + TOP, :] = blank


def partition_kernel(lengths, counts, types, low, high, q, back, fields, out, w, total):
    planes, nx, ny = q.shape
    depth = low.shape[1]
    cls = own_class()
    size = size_of(lengths, counts, cls)
    spread = diffusion_scale * size
    keep = 1.0 - 6.0 * spread
    scale = -0.5 * size
    kind = types[cls, 0]
    edge_low, edge_high = lane_edges(nx, ny)
    clear_margins(w, nx)
    w[0, 0, TOP : TOP + nx, :] = jnp.exp(scale * low[1 + kind, depth - 1]) * low[0, depth - 1]
    w[0, planes + 1, TOP : TOP + nx, :] = jnp.exp(scale * high[1 + kind, 0]) * high[0, 0]

    def weigh(p, carry):
        start = q[p].astype(jnp.float32)
        w[0, p + 1, TOP : TOP + nx, :] = jnp.exp(scale * fields[kind, p]) * start
        return carry

    lax.fori_loop(0, planes, weigh, 0, unroll=2)
    total[...] = jnp.zeros_like(total)

    def step(p, carry):
        core, beside = neighbours(w, 0, p + 1, edge_low, edge_high, nx)
        half = jnp.exp(scale * fields[kind, p])
        fresh = half * (keep * core + spread * beside)
        total[...] += folded(fresh * back[0, p].astype(jnp.float32))
        return carry

    lax.fori_loop(0, planes, step, 0, unroll=2)
    out[...] = jnp.broadcast_to(total[...][None], out.shape)


def main_kernel(
    lengths, counts, types, low, high, q, back, fields, final, dens, sums, half, w, total
):
    planes, nx, ny = q.shape
    depth = low.shape[1]
    wide = planes + 2 * depth
    cls = own_class()
    slab = lax.axis_index(SLAB)
    inner_low = splat(jnp.where(slab > 0, 1.0, 0.0))
    inner_high = splat(jnp.where(slab < lax.axis_size(SLAB) - 1, 1.0, 0.0))
    size = size_of(lengths, counts, cls)
    spread = diffusion_scale * size
    keep = 1.0 - 6.0 * spread
    scale = -0.5 * size
    kinds = [types[cls, s] for s in range(depth)]
    edge_low, edge_high = lane_edges(nx, ny)
    clear_margins(w, nx)
    total[...] = jnp.zeros_like(total)
    rows = slice(TOP, TOP + nx)

    for p in range(depth):
        for t in range(2):
            half[t, p] = jnp.exp(scale * low[1 + t, p])
            half[t, depth + planes + p] = jnp.exp(scale * high[1 + t, p])
        w[0, p, rows, :] = half[kinds[0], p] * low[0, p]
        w[0, depth + planes + p, rows, :] = half[kinds[0], depth + planes + p] * high[0, p]

    def first(p, carry):
        half[0, depth + p] = jnp.exp(scale * fields[0, p])
        half[1, depth + p] = jnp.exp(scale * fields[1, p])
        w[0, depth + p, rows, :] = half[kinds[0], depth + p] * q[p].astype(jnp.float32)
        dens[p, 0] = jnp.zeros((nx, ny), jnp.float32)
        dens[p, 1] = jnp.zeros((nx, ny), jnp.float32)
        return carry

    lax.fori_loop(0, planes, first, 0, unroll=2)

    for s in range(depth):
        now, later = s % 2, (s + 1) % 2
        kind = kinds[s]
        last = s == depth - 1

        def fresh_of(p):
            core, beside = neighbours(w, now, p, edge_low, edge_high, nx)
            return half[kind, p] * (keep * core + spread * beside)

        for p in range(s + 1, depth):
            far = wide - 1 - p
            w[later, p, rows, :] = half[kinds[s + 1], p] * (inner_low * fresh_of(p))
            w[later, far, rows, :] = half[kinds[s + 1], far] * (inner_high * fresh_of(far))

        def middle(p, carry):
            fresh = fresh_of(p + depth)
            product = fresh * back[s, p].astype(jnp.float32)
            dens[p, kind] += product
            total[...] += folded(product)
            if last:
                final[p] = fresh.astype(jnp.bfloat16)
            else:
                w[later, p + depth, rows, :] = half[kinds[s + 1], p + depth] * fresh
            return carry

        lax.fori_loop(0, planes, middle, 0, unroll=2)
    sums[...] = total[...]


def weigh_kernel(cells, lengths, counts, parts, dens, sums, out):
    planes, _, nx, ny = dens.shape
    cls = own_class()
    size = size_of(lengths, counts, cls)
    whole = lengths[0]
    for c in range(1, lengths.shape[0]):
        whole = whole + lengths[c]
    fraction = splat(lengths[cls].astype(jnp.float32)) / splat(whole.astype(jnp.float32))
    partition = jnp.sum(parts[...]) / cells
    weight = fraction * size / splat(partition)
    extra = weight * sums[...]

    def body(p, carry):
        out[p, 0:nx, :] = weight * dens[p, 0]
        out[p, nx : 2 * nx, :] = weight * dens[p, 1]
        out[p, 2 * nx : 2 * nx + 8, :] = extra
        return carry

    lax.fori_loop(0, planes, body, 0, unroll=2)


def reduce_kernel(arrived, out):
    acc = arrived[0]
    for c in range(1, arrived.shape[0]):
        acc = acc + arrived[c]
    out[...] = acc


def spread_kernel(own, other, blocks, levels):
    both = own[...] + other[...]
    n = blocks.shape[1]
    blocks[...] = jnp.broadcast_to(both[None, :n], blocks.shape)
    levels[...] = jnp.broadcast_to(both[None, n:], levels.shape)


def update_kernel(cells, blocks, levels, fields, out):
    _, planes, nx, ny = fields.shape
    level = splat(jnp.sum(levels[...]) / cells)

    def body(p, carry):
        first, second = blocks[p, 0:nx, :], blocks[p, nx : 2 * nx, :]
        pressure = stiffness * (first + second - level)
        old = fields[0, p]
        out[0, p] = old + mixing * (flory_chi * second + pressure - old)
        old = fields[1, p]
        out[1, p] = old + mixing * (flory_chi * first + pressure - old)
        return carry

    lax.fori_loop(0, planes, body, 0, unroll=2)


def call(kernel, outs, scratch, args, smem, flops, name):
    size = sum(a.size * a.dtype.itemsize for a in args) + sum(
        o.size * o.dtype.itemsize for o in outs
    )
    return pl.pallas_call(
        kernel,
        out_shape=outs,
        in_specs=[SMEM] * smem + [VMEM] * (len(args) - smem),
        out_specs=[VMEM] * len(outs),
        scratch_shapes=scratch,
        compiler_params=pltpu.CompilerParams(vmem_limit_bytes=24 * 2**20),
        cost_estimate=pl.CostEstimate(flops=flops, bytes_accessed=size, transcendentals=0),
        name=name,
    )(*args)


def f32(*shape):
    return jax.ShapeDtypeStruct(shape, jnp.float32)


def swapped(x, axis, shift):
    count = lax.axis_size(axis)
    pairs = [(i, i + shift) for i in range(count) if 0 <= i + shift < count]
    return lax.ppermute(x, axis, pairs)


def body(q_init, q_back, fields, lengths, counts, types):
    _, planes, nx, ny = q_init.shape
    depth = q_back.shape[1]
    cells = float(lax.axis_size(SLAB) * planes * nx * ny)
    q, back = q_init[0], q_back[0]
    peers = lax.axis_size(XY)
    slabs = lax.axis_size(SLAB)

    def edge(start):
        own = lax.slice_in_dim(q, start, start + depth, axis=0).astype(jnp.float32)
        return jnp.concatenate(
            [own[None], lax.slice_in_dim(fields, start, start + depth, axis=1)], 0
        )

    low = swapped(edge(planes - depth), SLAB, 1)
    high = swapped(edge(0), SLAB, -1)

    padded = nx + 2 * TOP
    ins = (lengths, counts, types, low, high, q, back, fields)
    (parts,) = call(
        partition_kernel,
        [f32(slabs, 8, ny)],
        [pltpu.VMEM((1, planes + 2, padded, ny), jnp.float32), pltpu.VMEM((8, ny), jnp.float32)],
        ins,
        3,
        10**6,
        "partition",
    )
    parts = lax.all_to_all(parts, SLAB, 0, 0, tiled=True)
    wide = planes + 2 * depth
    final, dens, sums = call(
        main_kernel,
        [
            jax.ShapeDtypeStruct((planes, nx, ny), jnp.bfloat16),
            f32(planes, 2, nx, ny),
            f32(8, ny),
        ],
        [
            pltpu.VMEM((2, wide, nx, ny), jnp.float32),
            pltpu.VMEM((2, wide, padded, ny), jnp.float32),
            pltpu.VMEM((8, ny), jnp.float32),
        ],
        ins,
        3,
        10**8,
        "propagate",
    )
    (sent,) = call(
        functools.partial(weigh_kernel, cells),
        [f32(peers, 2 * nx + 8, ny)],
        [],
        (lengths, counts, parts, dens, sums),
        2,
        10**6,
        "weigh",
    )
    arrived = lax.all_to_all(sent, XY, 0, 0, tiled=True)
    (own,) = call(reduce_kernel, [f32(2 * nx + 8, ny)], [], (arrived,), 0, 10**6, "reduce")
    other = lax.ppermute(own, "zh", [(0, 1), (1, 0)])
    blocks, levels = call(
        spread_kernel,
        [f32(peers, 2 * nx, ny), f32(slabs, 8, ny)],
        [],
        (own, other),
        0,
        10**6,
        "spread",
    )
    levels = lax.all_to_all(levels, SLAB, 0, 0, tiled=True)
    blocks = lax.all_to_all(blocks, XY, 0, 0, tiled=True)
    (fields_new,) = call(
        functools.partial(update_kernel, cells),
        [f32(2, planes, nx, ny)],
        [],
        (blocks, levels, fields),
        0,
        10**6,
        "update",
    )
    return fields_new, final[None]


def solution(mesh):
    finer = Mesh(mesh.devices.reshape(2, 4, 4, mesh.shape["slab"]), ("zh", "y", "x", SLAB))
    in_specs = (
        P(CLS, SLAB, None, None),
        P(CLS, None, SLAB, None, None),
        P(None, SLAB, None, None),
        P(),
        P(),
        P(),
    )
    out_specs = (P(None, SLAB, None, None), P(CLS, SLAB, None, None))
    return jax.shard_map(body, mesh=finer, in_specs=in_specs, out_specs=out_specs, check_vma=False)
```

time: 144 us -> 125 us (0.87)
  blocking collectives: 90.2 us -> 64.6 us
  Pallas kernels: 0 us -> 10.7 us
  other arithmetic: 12.6 us -> 2.45 us
  starting transfers between devices: 19.6 us -> 29.3 us
  between operations: 8.37 us -> 0.76 us
  waiting for transfers between devices: 7.9 us -> 13.1 us
  local copies, waits for them, and re-layouts: 5.13 us -> 3.54 us
    all_to_all x5 -> x3, blocking collectives: 90.2 us -> 64.6 us  [the longest x1 23.3 us: body(): arrived = lax.all_to_all(sent, XY, 0, 0, tiled=True)]
    pallas_call x0 -> x6, Pallas kernels: none -> 10.7 us  [call(): pl.pallas_call(kernel, out_shape=outs, in_specs=[SMEM] * smem + [VMEM] *...]
    ppermute x2 -> x3, waiting for transfers between devices: 0.01 us -> 9.98 us  [the longest x1 5.92 us: body(): other = lax.ppermute(own, 'zh', [(0, 1), (1, 0)])]
    ppermute x2 -> x3, starting transfers between devices: 10.1 us -> 18 us  [the longest x2 10 us: swapped(): return lax.ppermute(x, axis, pairs)]
    all_to_all x1, waiting for transfers between devices: 7.89 us -> 3.15 us  [body(): parts = lax.all_to_all(parts, SLAB, 0, 0, tiled=True)]
    mul x6 -> x0, other arithmetic: 4.57 us -> none  [the longest x2 2.44 us: body(): factor = weight[:, None] * select]
    reduce_sum x6 -> x0, other arithmetic: 2.66 us -> none  [the longest x2 1.23 us: over_copies(): return jnp.sum(everything, axis=0)]
    broadcast_in_dim x4 -> x0, local copies, waits for them, and re-layouts: 1.93 us -> none  [sent_to_all(): jnp.broadcast_to(x[None], (peers, *x.shape))]
  transfers between devices with their start and end apart: 3 -> 4, of which waited for: 1 -> 3; matrix products, arithmetic and copies ran while one was open for 2% -> 1% of each run, Pallas kernels for 0% -> 5%
where the time goes in v1:
time: 125 us; the launch traced here: 124 us
  blocking collectives  64.6 us (52%)
  starting transfers between devices  29.3 us (23%)
  waiting for transfers between devices  13.1 us (10%)
  Pallas kernels  10.7 us (9%)
  local copies, waits for them, and re-layouts  3.54 us (3%)
  other arithmetic  2.45 us (2%)
    all_to_all x1, blocking collectives, body(): arrived = lax.all_to_all(sent, XY, 0, 0, tiled=True)  23.3 us
    all_to_all x1, blocking collectives, body(): levels = lax.all_to_all(levels, SLAB, 0, 0, tiled=True)  20.8 us
    all_to_all x1, blocking collectives, body(): blocks = lax.all_to_all(blocks, XY, 0, 0, tiled=True)  20.6 us
    all_to_all x1, starting transfers between devices, body(): parts = lax.all_to_all(parts, SLAB, 0, 0, tiled=True)  11.3 us
    pallas_call x6, Pallas kernels, call(): pl.pallas_call(kernel, out_shape=outs, in_specs=[SMEM] * smem + [VMEM] *...  10.7 us
    ppermute x2, starting transfers between devices, swapped(): return lax.ppermute(x, axis, pairs)  10 us
    ppermute x1, starting transfers between devices, body(): other = lax.ppermute(own, 'zh', [(0, 1), (1, 0)])  7.94 us
    ppermute x1, waiting for transfers between devices, body(): other = lax.ppermute(own, 'zh', [(0, 1), (1, 0)])  5.92 us
  transfers between devices with their start and end apart: 4, of which 3 were waited for; matrix products, arithmetic and copies ran while one was open for 1% of the time, Pallas kernels for 5%

profile of v1, /device:TPU:1, one launch (start us, length us, event | category | flops | bytes accessed | tf_op | source)
XLA Modules:
  0.0 124.5 jit_solution(7486877192039788463)
XLA Ops:
  0.6 0.9 slice_convert_fusion
  1.5 0.0 copy-start.1
  1.6 1.2 fusion
  2.8 0.8 pad_maximum_fusion
  3.6 4.9 %collective-permute-start = (f32[3,4,64,128]{3,2,1,0:T(8,128)}, f32[3,4,64,128]{3,2,1,0:T(8,128)S(1)}, u32[]{:S(2)}, u32[]{:S(2)}) collective-permute-start(f32[3,4,64,128]{3,2,1,0:T(8,128)} %pad_maximum_fusion), channel_id=1, source_target_pairs={{0,1},{1,2},{2,3},{3,4},{4,5},{5,6},{6,7},{7,8},{8,9},{9,10},{10,1... | collective-permute-start | bytes 1179656 | tf_op jit(solution)/shard_map/ppermute | solution.py:235
  8.5 0.8 pad_maximum_fusion.1
  9.3 5.1 %collective-permute-start.1 = (f32[3,4,64,128]{3,2,1,0:T(8,128)}, f32[3,4,64,128]{3,2,1,0:T(8,128)S(1)}, u32[]{:S(2)}, u32[]{:S(2)}) collective-permute-start(f32[3,4,64,128]{3,2,1,0:T(8,128)} %pad_maximum_fusion.1), channel_id=1, source_target_pairs={{1,0},{2,1},{3,2},{4,3},{5,4},{6,5},{7,6},{8,7},{9,8},{10,9},{11,1... | collective-permute-start | bytes 1179656 | tf_op jit(solution)/shard_map/ppermute | solution.py:235
  14.4 0.1 copy.8.types
  14.5 4.1 %collective-permute-done.1.high = f32[3,4,64,128]{3,2,1,0:T(8,128)S(1)} collective-permute-done((f32[3,4,64,128]{3,2,1,0:T(8,128)}, f32[3,4,64,128]{3,2,1,0:T(8,128)S(1)}, u32[]{:S(2)}, u32[]{:S(2)}) %collective-permute-start.1) | collective-permute-done | bytes 393248 | tf_op jit(solution)/shard_map/ppermute | solution.py:235
  18.6 2.5 %partition.1 = f32[16,8,128]{2,1,0:T(8,128)} custom-call(s32[32]{0:T(128)S(1)} %copy-done.5, s32[32]{0:T(128)S(1)} %copy-done.6, s32[32,4]{1,0:T(8,128)S(1)} %copy.8.types, f32[3,4,64,128]{3,2,1,0:T(8,128)S(1)} %collective-permute-done.low, f32[3,4,64,128]{3,2,1,0:T(8,128)S(1)} %collective-permute-done.1.high, bf16[16,64,128]{2,1,0:T(8,128)(2,1)S(1)} %bitcast.5, ...), custom_call_target="tpu_custom_call" | custom-call | flops 1000000 | bytes 3212032 | tf_op jit(solution)/shard_map/partition/pallas_call | solution.py:216
  21.2 11.3 %all-to-all-start = ((f32[16,8,128]{2,1,0:T(8,128)}), f32[16,8,128]{2,1,0:T(8,128)S(1)}, u32[]{:S(2)}, u32[]{:S(2)}) async-start(f32[16,8,128]{2,1,0:T(8,128)} %partition.1), calls=%async_computation | async-start | bytes 131072 | tf_op jit(solution)/shard_map/all_to_all | solution.py:266
  32.5 5.9 %propagate.1 = (bf16[16,64,128]{2,1,0:T(8,128)(2,1)}, f32[16,2,64,128]{3,2,1,0:T(8,128)S(1)}, f32[8,128]{1,0:T(8,128)S(1)}) custom-call(s32[32]{0:T(128)S(1)} %copy-done.5, s32[32]{0:T(128)S(1)} %copy-done.6, s32[32,4]{1,0:T(8,128)S(1)} %copy.8.types, f32[3,4,64,128]{3,2,1,0:T(8,128)S(1)} %collective-permute-done.low, ...), custom_call_target="tpu_custom_call" | custom-call | flops 100000000 | bytes 4461312 | tf_op jit(solution)/shard_map/propagate/pallas_call | solution.py:216
  38.4 1.0 copy-done.3
  39.3 3.2 %all-to-all-done.parts = f32[16,8,128]{2,1,0:T(8,128)S(1)} async-done(((f32[16,8,128]{2,1,0:T(8,128)}), f32[16,8,128]{2,1,0:T(8,128)S(1)}, u32[]{:S(2)}, u32[]{:S(2)}) %all-to-all-start) | async-done | bytes 65568 | tf_op jit(solution)/shard_map/all_to_all | solution.py:266
  42.5 1.2 copy-done.4
  43.7 0.8 weigh.1
  44.5 23.3 %all_to_all.20.arrived = f32[16,136,128]{2,1,0:T(8,128)S(1)} all-to-all(f32[16,136,128]{2,1,0:T(8,128)S(1)} %weigh.1), channel_id=1, replica_groups=mesh['zh'=2,'y'=4,'x'=4,'slab'=16] {'y','x'}, dimensions={0} | all-to-all | bytes 2228224 | tf_op jit(solution)/shard_map/all_to_all | solution.py:294
  67.8 0.1 reduce.1.own
  67.8 7.9 %collective-permute-start.2 = (f32[136,128]{1,0:T(8,128)S(1)}, f32[136,128]{1,0:T(8,128)S(1)}, u32[]{:S(2)}, u32[]{:S(2)}) collective-permute-start(f32[136,128]{1,0:T(8,128)S(1)} %reduce.1.own), channel_id=1, source_target_pairs={{0,256},{256,0},{1,257},{257,1},{2,258},{258,2},{3,259},{259,3},{4... | collective-permute-start | bytes 208904 | tf_op jit(solution)/shard_map/ppermute | solution.py:296
  75.8 5.9 %collective-permute-done.2.other = f32[136,128]{1,0:T(8,128)S(1)} collective-permute-done((f32[136,128]{1,0:T(8,128)S(1)}, f32[136,128]{1,0:T(8,128)S(1)}, u32[]{:S(2)}, u32[]{:S(2)}) %collective-permute-start.2) | collective-permute-done | bytes 69664 | tf_op jit(solution)/shard_map/ppermute | solution.py:296
  81.7 0.1 spread.1
  81.8 20.8 %all_to_all.21.levels = f32[16,8,128]{2,1,0:T(8,128)S(1)} all-to-all(f32[16,8,128]{2,1,0:T(8,128)S(1)} %get-tuple-element.10), channel_id=1, replica_groups=mesh['zh'=2,'y'=4,'x'=4,'slab'=16] {'slab'}, dimensions={0} | all-to-all | bytes 131072 | tf_op jit(solution)/shard_map/all_to_all | solution.py:306
  102.6 20.6 %all_to_all.22.blocks = f32[16,128,128]{2,1,0:T(8,128)S(1)} all-to-all(f32[16,128,128]{2,1,0:T(8,128)S(1)} %get-tuple-element.9), channel_id=1, replica_groups=mesh['zh'=2,'y'=4,'x'=4,'slab'=16] {'y','x'}, dimensions={0} | all-to-all | bytes 2097152 | tf_op jit(solution)/shard_map/all_to_all | solution.py:307
  123.1 1.3 %update.1 = f32[2,16,64,128]{3,2,1,0:T(8,128)} custom-call(f32[16,128,128]{2,1,0:T(8,128)S(1)} %all_to_all.22.blocks, f32[16,8,128]{2,1,0:T(8,128)S(1)} %all_to_all.21.levels, f32[2,16,64,128]{3,2,1,0:T(8,128)S(1)} %copy-done), custom_call_target="tpu_custom_call" | custom-call | flops 1000000 | bytes 3211264 | tf_op jit(solution)/shard_map/update/pallas_call | solution.py:216
  (14 shorter events, 0.0 us)
Async XLA Ops:
  1.5 12.9 %copy-start.7 = (s32[32,4]{0,1:T(4,128)S(1)}, s32[32,4]{0,1:T(4,128)}, u32[]{:S(2)}) copy-start(s32[32,4]{0,1:T(4,128)} %param.11) | copy-start | bytes 1540
  1.5 17.1 %copy-start = (f32[2,16,64,128]{3,2,1,0:T(8,128)S(1)}, f32[2,16,64,128]{3,2,1,0:T(8,128)}, u32[]{:S(2)}) copy-start(f32[2,16,64,128]{3,2,1,0:T(8,128)} %fields.5) | copy-start | bytes 3145732
  1.5 17.1 %copy-start.1 = (bf16[1,4,16,64,128]{4,3,2,1,0:T(8,128)(2,1)S(1)}, bf16[1,4,16,64,128]{4,3,2,1,0:T(8,128)(2,1)}, u32[]{:S(2)}) copy-start(bf16[1,4,16,64,128]{4,3,2,1,0:T(8,128)(2,1)} %param.7) | copy-start | bytes 3145732
  1.6 17.0 %copy-start.2 = (bf16[1,16,64,128]{3,2,1,0:T(8,128)(2,1)S(1)}, bf16[1,16,64,128]{3,2,1,0:T(8,128)(2,1)}, u32[]{:S(2)}) copy-start(bf16[1,16,64,128]{3,2,1,0:T(8,128)(2,1)} %param.6) | copy-start | bytes 786436
  1.6 17.0 %copy-start.5 = (s32[32]{0:T(128)S(1)}, s32[32]{0:T(128)}, u32[]{:S(2)}) copy-start(s32[32]{0:T(128)} %lengths.5) | copy-start | bytes 388
  1.6 17.0 %copy-start.6 = (s32[32]{0:T(128)S(1)}, s32[32]{0:T(128)}, u32[]{:S(2)}) copy-start(s32[32]{0:T(128)} %counts.5) | copy-start | bytes 388
  3.6 10.9 %collective-permute-start = (f32[3,4,64,128]{3,2,1,0:T(8,128)}, f32[3,4,64,128]{3,2,1,0:T(8,128)S(1)}, u32[]{:S(2)}, u32[]{:S(2)}) collective-permute-start(f32[3,4,64,128]{3,2,1,0:T(8,128)} %pad_maximum_fusion), channel_id=1, source_target_pairs={{0,1},{1,2},{2,3},{3,4},{4,5},{5,6},{6,7},{7,8},{8,9},{9,10},{10,1... | collective-permute-start | bytes 1179656 | tf_op jit(solution)/shard_map/ppermute | solution.py:235
  9.3 9.3 %collective-permute-start.1 = (f32[3,4,64,128]{3,2,1,0:T(8,128)}, f32[3,4,64,128]{3,2,1,0:T(8,128)S(1)}, u32[]{:S(2)}, u32[]{:S(2)}) collective-permute-start(f32[3,4,64,128]{3,2,1,0:T(8,128)} %pad_maximum_fusion.1), channel_id=1, source_target_pairs={{1,0},{2,1},{3,2},{4,3},{5,4},{6,5},{7,6},{8,7},{9,8},{10,9},{11,1... | collective-permute-start | bytes 1179656 | tf_op jit(solution)/shard_map/ppermute | solution.py:235
  21.2 21.3 %all-to-all-start = ((f32[16,8,128]{2,1,0:T(8,128)}), f32[16,8,128]{2,1,0:T(8,128)S(1)}, u32[]{:S(2)}, u32[]{:S(2)}) async-start(f32[16,8,128]{2,1,0:T(8,128)} %partition.1), calls=%async_computation | async-start | bytes 131072 | tf_op jit(solution)/shard_map/all_to_all | solution.py:266
  38.4 1.0 copy-start.3
  42.5 1.2 copy-start.4
  67.8 13.9 %collective-permute-start.2 = (f32[136,128]{1,0:T(8,128)S(1)}, f32[136,128]{1,0:T(8,128)S(1)}, u32[]{:S(2)}, u32[]{:S(2)}) collective-permute-start(f32[136,128]{1,0:T(8,128)S(1)} %reduce.1.own), channel_id=1, source_target_pairs={{0,256},{256,0},{1,257},{257,1},{2,258},{258,2},{3,259},{259,3},{4... | collective-permute-start | bytes 208904 | tf_op jit(solution)/shard_map/ppermute | solution.py:296

commit v2 on v1

v2 whole, which is shorter than its diff:
```python
import functools

import jax
import jax.numpy as jnp
from jax import lax
from jax.experimental import pallas as pl
from jax.experimental.pallas import tpu as pltpu
from jax.sharding import Mesh
from jax.sharding import PartitionSpec as P

CLS = ("zh", "y", "x")
XY = ("y", "x")
SLAB = "slab"

flory_chi = 2.0
stiffness = 1.0
mixing = 0.5
diffusion_scale = 0.125

VMEM = pl.BlockSpec(memory_space=pltpu.VMEM)
SMEM = pl.BlockSpec(memory_space=pltpu.SMEM)
TOP = 8


def own_class():
    return (lax.axis_index("zh") * 4 + lax.axis_index("y")) * 4 + lax.axis_index("x")


def splat(value, shape=(1, 128)):
    return jnp.full(shape, value, jnp.float32)


def size_of(lengths, counts, cls):
    return splat(lengths[cls].astype(jnp.float32)) / splat(counts[cls].astype(jnp.float32))


def folded(plane):
    return jnp.sum(plane.reshape(-1, 8, plane.shape[-1]), axis=0)


def neighbours(w, at, p, lane_low, lane_high, nx):
    core = w[(*at, p, slice(TOP, TOP + nx))]
    total = w[(*at, p - 1, slice(TOP, TOP + nx))] + w[(*at, p + 1, slice(TOP, TOP + nx))]
    total = total + w[(*at, p, slice(TOP - 1, TOP + nx - 1))]
    total = total + w[(*at, p, slice(TOP + 1, TOP + nx + 1))]
    ny = core.shape[-1]
    before = jnp.where(lane_low, 0.0, pltpu.roll(core, 1, 1))
    after = jnp.where(lane_high, 0.0, pltpu.roll(core, ny - 1, 1))
    return core, total + before + after


def lane_edges(nx, ny):
    lane = lax.broadcasted_iota(jnp.int32, (nx, ny), 1)
    return lane == 0, lane == ny - 1


def clear_margins(w, nx):
    blank = jnp.zeros(w.shape[:2] + (TOP, w.shape[-1]), jnp.float32)
    w[:, :, 0:TOP, :] = blank
    w[:, :, TOP + nx : TOP + nx + TOP, :] = blank


def edges_kernel(lengths, counts, types, q, fields, up, down, ends, sems):
    planes = q.shape[0]
    depth = types.shape[0]
    cls = own_class()
    kind = types[0, cls]
    rest = depth - 1
    copies = []
    for side, start in enumerate((planes - depth, 0)):
        copies.append((q.at[pl.ds(start, depth)], ends.at[side]))
    for t in range(2):
        at = pl.ds(depth + t * rest, rest)
        copies.append((fields.at[t, pl.ds(planes - rest, rest)], up.at[at]))
        copies.append((fields.at[t, pl.ds(0, rest)], down.at[at]))
    copies.append((fields.at[kind, pl.ds(planes - depth, 1)], up.at[pl.ds(0, 1)]))
    copies.append((fields.at[kind, pl.ds(rest, 1)], down.at[pl.ds(rest, 1)]))
    copies = [pltpu.make_async_copy(a, b, sems.at[i]) for i, (a, b) in enumerate(copies)]
    for copy in copies:
        copy.start()
    for copy in copies:
        copy.wait()
    scale = -0.5 * size_of(lengths, counts, cls)
    ours = depth + kind * rest
    for p in range(depth):
        chosen = up[0] if p == 0 else up[ours + p - 1]
        up[p] = jnp.exp(scale * chosen) * ends[0, p].astype(jnp.float32)
        chosen = down[rest] if p == rest else down[ours + p]
        down[p] = jnp.exp(scale * chosen) * ends[1, p].astype(jnp.float32)


def inner_kernel(
    lengths, counts, types, q, back, fields, half, state, dens, middle, sums, w, total
):
    planes, nx, ny = q.shape
    depth = back.shape[0]
    cls = own_class()
    size = size_of(lengths, counts, cls)
    spread = diffusion_scale * size
    keep = 1.0 - 6.0 * spread
    scale = -0.5 * size
    kinds = [types[s, cls] for s in range(depth)]
    edge_low, edge_high = lane_edges(nx, ny)
    clear_margins(w, nx)
    total[...] = jnp.zeros_like(total)
    rows = slice(TOP, TOP + nx)

    def first(p, carry):
        half[0, p] = jnp.exp(scale * fields[0, p])
        half[1, p] = jnp.exp(scale * fields[1, p])
        w[0, p, rows, :] = half[kinds[0], p] * q[p].astype(jnp.float32)
        dens[p, 0] = jnp.zeros((nx, ny), jnp.float32)
        dens[p, 1] = jnp.zeros((nx, ny), jnp.float32)
        return carry

    lax.fori_loop(0, planes, first, 0, unroll=2)

    for s in range(depth):
        now, later = s % 2, (s + 1) % 2
        kind = kinds[s]
        last = s == depth - 1
        for i, p in enumerate((s, s + 1, planes - 1 - s, planes - 2 - s)):
            state[s, i] = w[now, p, rows, :]

        def each(p, carry):
            core, beside = neighbours(w, (now,), p, edge_low, edge_high, nx)
            fresh = half[kind, p] * (keep * core + spread * beside)
            product = fresh * back[s, p].astype(jnp.float32)
            dens[p, kind] += product
            total[...] += folded(product)
            if last:
                middle[p - depth] = fresh.astype(jnp.bfloat16)
            else:
                w[later, p, rows, :] = half[kinds[s + 1], p] * fresh
            return carry

        lax.fori_loop(s + 1, planes - 1 - s, each, 0, unroll=2)
        if s == 0:
            sums[0] = total[...]
    sums[1] = total[...]


def outer_kernel(
    lengths,
    counts,
    types,
    low,
    high,
    back,
    half,
    state,
    dens,
    middle,
    inner_sums,
    final,
    edge_dens,
    sums,
    w,
    total,
):
    planes, nx, ny = final.shape
    depth = back.shape[0]
    cls = own_class()
    slab = lax.axis_index(SLAB)
    inside = (
        splat(jnp.where(slab > 0, 1.0, 0.0)),
        splat(jnp.where(slab < lax.axis_size(SLAB) - 1, 1.0, 0.0)),
    )
    size = size_of(lengths, counts, cls)
    spread = diffusion_scale * size
    keep = 1.0 - 6.0 * spread
    scale = -0.5 * size
    kinds = [types[s, cls] for s in range(depth)]
    edge_low, edge_high = lane_edges(nx, ny)
    for side in range(2):
        clear_margins(w.at[side], nx)
    total[...] = jnp.zeros_like(total)
    rows = slice(TOP, TOP + nx)
    came = (low, high)
    rest = depth - 1

    def half_of(side, r, kind):
        if r >= depth:
            return half[kind, r - depth if side == 0 else planes - 1 + depth - r]
        at = r - 1 if side == 0 else rest - r
        return jnp.exp(scale * came[side][depth + kind * rest + at])

    for side in range(2):
        for r in range(depth):
            w[side, 0, r, rows, :] = came[side][r if side == 0 else rest - r]
        for p in range(depth):
            at = p if side == 0 else planes - 1 - p
            for t in range(2):
                edge_dens[side * depth + p, t] = dens[at, t]

    for s in range(depth):
        now, later = s % 2, (s + 1) % 2
        for side in range(2):
            for i in range(2):
                w[side, now, s + depth + i, rows, :] = state[s, 2 * side + i]
        for i in range(depth):
            for side in range(2):
                r = s + 1 + i
                core, beside = neighbours(w, (side, now), r, edge_low, edge_high, nx)
                fresh = half_of(side, r, kinds[s]) * (keep * core + spread * beside)
                if r < depth:
                    fresh = inside[side] * fresh
                else:
                    at = r - depth if side == 0 else planes - 1 + depth - r
                    product = fresh * back[s, at].astype(jnp.float32)
                    edge_dens[side * depth + r - depth, kinds[s]] += product
                    total[...] += folded(product)
                    if s == rest:
                        final[at] = fresh.astype(jnp.bfloat16)
                if s < rest:
                    w[side, later, r, rows, :] = half_of(side, r, kinds[s + 1]) * fresh
        if s == 0:
            part = inner_sums[0] + total[...]
            sums[:, 0:8] = jnp.broadcast_to(part[None], (sums.shape[0], 8, ny))
    whole = inner_sums[1] + total[...]
    sums[:, 8:16] = jnp.broadcast_to(whole[None], (sums.shape[0], 8, ny))
    for p in range(planes - 2 * depth):
        final[depth + p] = middle[p]


def weigh_kernel(cells, lengths, counts, sums, dens, edge_dens, out, extra):
    planes, _, nx, ny = dens.shape
    depth = edge_dens.shape[0] // 2
    cls = own_class()
    size = size_of(lengths, counts, cls)
    whole = lengths[0]
    for c in range(1, lengths.shape[0]):
        whole = whole + lengths[c]
    fraction = splat(lengths[cls].astype(jnp.float32)) / splat(whole.astype(jnp.float32))
    both = jnp.sum(sums[...], axis=0)
    partition = jnp.sum(both[0:8]) / cells
    weight = fraction * size / splat(partition)
    extra[...] = weight * both[8:16]

    def body(p, carry):
        for t in range(2):
            out[p, t * nx : (t + 1) * nx, :] = weight * dens[p, t]
        return carry

    lax.fori_loop(depth, planes - depth, body, 0, unroll=2)

    def ends(p, carry):
        for t in range(2):
            out[p, t * nx : (t + 1) * nx, :] = weight * edge_dens[p, t]
            out[planes - 1 - p, t * nx : (t + 1) * nx, :] = weight * edge_dens[depth + p, t]
        return carry

    lax.fori_loop(0, depth, ends, 0)


def reduce_kernel(arrived, extra, out):
    acc = arrived[0]
    for c in range(1, arrived.shape[0]):
        acc = acc + arrived[c]
    out[0 : acc.shape[0]] = acc
    out[acc.shape[0] :] = extra[...]


def spread_kernel(own, other, blocks):
    both = own[...] + other[...]
    blocks[...] = jnp.broadcast_to(both[None], blocks.shape)


def update_kernel(cells, blocks, fields, out):
    _, planes, nx, ny = fields.shape
    level = splat(jnp.sum(jnp.sum(blocks[:, 2 * nx :], axis=0)) / cells)

    def body(p, carry):
        first, second = blocks[p, 0:nx, :], blocks[p, nx : 2 * nx, :]
        pressure = stiffness * (first + second - level)
        old = fields[0, p]
        out[0, p] = old + mixing * (flory_chi * second + pressure - old)
        old = fields[1, p]
        out[1, p] = old + mixing * (flory_chi * first + pressure - old)
        return carry

    lax.fori_loop(0, planes, body, 0, unroll=2)


def call(kernel, outs, scratch, args, smem, flops, name, vmem=2, hbm=0):
    size = sum(a.size * a.dtype.itemsize for a in args) + sum(
        o.size * o.dtype.itemsize for o in outs
    )
    anywhere = pl.BlockSpec(memory_space=pltpu.HBM)
    return pl.pallas_call(
        kernel,
        out_shape=outs,
        in_specs=[SMEM] * smem + [VMEM] * (len(args) - smem - hbm) + [anywhere] * hbm,
        out_specs=[VMEM] * len(outs),
        scratch_shapes=scratch,
        compiler_params=pltpu.CompilerParams(vmem_limit_bytes=vmem and vmem * 2**20),
        cost_estimate=pl.CostEstimate(flops=flops, bytes_accessed=size, transcendentals=0),
        name=name,
    )(*args)


def f32(*shape):
    return jax.ShapeDtypeStruct(shape, jnp.float32)


def swapped(x, axis, shift):
    count = lax.axis_size(axis)
    pairs = [(i, i + shift) for i in range(count) if 0 <= i + shift < count]
    return lax.ppermute(x, axis, pairs)


def body(q_init, q_back, fields, lengths, counts, types):
    _, planes, nx, ny = q_init.shape
    depth = q_back.shape[1]
    cells = float(lax.axis_size(SLAB) * planes * nx * ny)
    q, back = q_init[0], q_back[0]
    types = types.T
    peers = lax.axis_size(XY)
    slabs = lax.axis_size(SLAB)
    message = f32(3 * depth - 2, nx, ny)

    up, down = call(
        edges_kernel,
        [message, message],
        [pltpu.VMEM((2, depth, nx, ny), jnp.bfloat16), pltpu.SemaphoreType.DMA((8,))],
        (lengths, counts, types, q, fields),
        3,
        10**6,
        "edges",
        vmem=None,
        hbm=2,
    )
    low = swapped(up, SLAB, 1)
    high = swapped(down, SLAB, -1)

    padded = nx + 2 * TOP
    half, state, dens, middle, sums = call(
        inner_kernel,
        [
            f32(2, planes, nx, ny),
            f32(depth, 4, nx, ny),
            f32(planes, 2, nx, ny),
            jax.ShapeDtypeStruct((planes - 2 * depth, nx, ny), jnp.bfloat16),
            f32(2, 8, ny),
        ],
        [
            pltpu.VMEM((2, planes, padded, ny), jnp.float32),
            pltpu.VMEM((8, ny), jnp.float32),
        ],
        (lengths, counts, types, q, back, fields),
        3,
        10**8,
        "inner",
        vmem=8,
    )
    final, edge_dens, sums = call(
        outer_kernel,
        [
            jax.ShapeDtypeStruct((planes, nx, ny), jnp.bfloat16),
            f32(2 * depth, 2, nx, ny),
            f32(slabs, 16, ny),
        ],
        [
            pltpu.VMEM((2, 2, 2 * depth + 2, padded, ny), jnp.float32),
            pltpu.VMEM((8, ny), jnp.float32),
        ],
        (lengths, counts, types, low, high, back, half, state, dens, middle, sums),
        3,
        10**8,
        "outer",
        vmem=8,
    )
    sums = lax.all_to_all(sums, SLAB, 0, 0, tiled=True)
    sent, extra = call(
        functools.partial(weigh_kernel, cells),
        [f32(peers, 2 * nx, ny), f32(8, ny)],
        [],
        (lengths, counts, sums, dens, edge_dens),
        2,
        10**6,
        "weigh",
        vmem=8,
    )
    arrived = lax.all_to_all(sent, XY, 0, 0, tiled=True)
    (own,) = call(
        reduce_kernel, [f32(2 * nx + 8, ny)], [], (arrived, extra), 0, 10**6, "reduce", vmem=8
    )
    other = lax.ppermute(own, "zh", [(0, 1), (1, 0)])
    (blocks,) = call(
        spread_kernel, [f32(peers, 2 * nx + 8, ny)], [], (own, other), 0, 10**6, "spread", vmem=8
    )
    blocks = lax.all_to_all(blocks, XY, 0, 0, tiled=True)
    (fields_new,) = call(
        functools.partial(update_kernel, cells),
        [f32(2, planes, nx, ny)],
        [],
        (blocks, fields),
        0,
        10**6,
        "update",
        vmem=8,
    )
    return fields_new, final[None]


def solution(mesh):
    finer = Mesh(mesh.devices.reshape(2, 4, 4, mesh.shape["slab"]), ("zh", "y", "x", SLAB))
    in_specs = (
        P(CLS, SLAB, None, None),
        P(CLS, None, SLAB, None, None),
        P(None, SLAB, None, None),
        P(),
        P(),
        P(),
    )
    out_specs = (P(None, SLAB, None, None), P(CLS, SLAB, None, None))
    return jax.shard_map(body, mesh=finer, in_specs=in_specs, out_specs=out_specs, check_vma=False)
```

time: 125 us -> 106 us (0.85)
  the two profiles are of different devices: /device:TPU:1 before, /device:TPU:32 now
where the time goes in v2:
time: 106 us; the launch traced here: 105 us
  blocking collectives  67.3 us (63%)
  starting transfers between devices  13.8 us (13%)
  waiting for transfers between devices  11.6 us (11%)
  Pallas kernels  10.7 us (10%)
  local copies, waits for them, and re-layouts  1.24 us (1%)
    all_to_all x1, blocking collectives, body(): arrived = lax.all_to_all(sent, XY, 0, 0, tiled=True)  24.8 us
    all_to_all x1, blocking collectives, body(): sums = lax.all_to_all(sums, SLAB, 0, 0, tiled=True)  22 us
    all_to_all x1, blocking collectives, body(): blocks = lax.all_to_all(blocks, XY, 0, 0, tiled=True)  20.6 us
    ppermute x1, waiting for transfers between devices, body(): other = lax.ppermute(own, 'zh', [(0, 1), (1, 0)])  11.5 us
    pallas_call x7, Pallas kernels, call(): pl.pallas_call(kernel, out_shape=outs, in_specs=[SMEM] * smem + [VMEM] *...  10.7 us
    ppermute x1, starting transfers between devices, body(): other = lax.ppermute(own, 'zh', [(0, 1), (1, 0)])  8.22 us
    ppermute x2, starting transfers between devices, swapped(): return lax.ppermute(x, axis, pairs)  5.56 us
  transfers between devices with their start and end apart: 3, of which 2 were waited for; matrix products, arithmetic and copies ran while one was open for 0% of the time, Pallas kernels for 3%

profile of v2, /device:TPU:32, one launch (start us, length us, event | category | flops | bytes accessed | tf_op | source)
XLA Modules:
  0.0 105.4 jit_solution(5877375912060652062)
XLA Ops:
  0.6 0.0 copy-start.6
  0.6 0.0 copy-start.5
  0.7 0.0 copy-start
  0.7 0.0 copy-start.4
  0.7 0.0 copy-start.3
  0.7 2.9 %edges.1 = (f32[10,64,128]{2,1,0:T(8,128)}, f32[10,64,128]{2,1,0:T(8,128)}) custom-call(s32[32]{0:T(128)} %lengths.7, s32[32]{0:T(128)} %counts.7, s32[4,32]{1,0:T(4,128)} %bitcast.8, bf16[16,64,128]{2,1,0:T(8,128)(2,1)} %bitcast.6, f32[2,16,64,128]{3,2,1,0:T(8,128)} %fields.5), custom_call_target="tpu_custom_call" | custom-call | flops 1000000 | bytes 1966848 | tf_op jit(solution)/shard_map/edges/pallas_call | solution.py:290
  3.6 1.9 %collective-permute-start = (f32[10,64,128]{2,1,0:T(8,128)}, f32[10,64,128]{2,1,0:T(8,128)S(1)}, u32[]{:S(2)}, u32[]{:S(2)}) collective-permute-start(f32[10,64,128]{2,1,0:T(8,128)} %get-tuple-element.14), channel_id=1, source_target_pairs={{0,1},{1,2},{2,3},{3,4},{4,5},{5,6},{6,7},{7,8},{8,9},{9,10},{10,1... | collective-permute-start | bytes 983048 | tf_op jit(solution)/shard_map/ppermute | solution.py:309
  5.5 3.6 %collective-permute-start.1 = (f32[10,64,128]{2,1,0:T(8,128)}, f32[10,64,128]{2,1,0:T(8,128)S(1)}, u32[]{:S(2)}, u32[]{:S(2)}) collective-permute-start(f32[10,64,128]{2,1,0:T(8,128)} %get-tuple-element.15), channel_id=1, source_target_pairs={{1,0},{2,1},{3,2},{4,3},{5,4},{6,5},{7,6},{8,7},{9,8},{10,9},{11,1... | collective-permute-start | bytes 983048 | tf_op jit(solution)/shard_map/ppermute | solution.py:309
  9.2 0.0 copy-start.1
  9.2 1.2 %copy-done.1 = bf16[1,4,16,64,128]{4,3,2,1,0:T(8,128)(2,1)S(1)} copy-done((bf16[1,4,16,64,128]{4,3,2,1,0:T(8,128)(2,1)S(1)}, bf16[1,4,16,64,128]{4,3,2,1,0:T(8,128)(2,1)}, u32[]{:S(2)}) %copy-start.1) | copy-done | bytes 1048600
  10.5 3.5 %inner.1 = (f32[2,16,64,128]{3,2,1,0:T(8,128)S(1)}, f32[4,4,64,128]{3,2,1,0:T(8,128)S(1)}, f32[16,2,64,128]{3,2,1,0:T(8,128)S(1)}, bf16[8,64,128]{2,1,0:T(8,128)(2,1)S(1)}, f32[2,8,128]{2,1,0:T(8,128)S(1)}) custom-call(s32[32]{0:T(128)S(1)} %copy-done.5, s32[32]{0:T(128)S(1)} %copy-done.6, s32[4,32]{1,0:T(4,128)S(1)} %bitcast.9, ...), custom_call_target="tpu_custom_call" | custom-call | flops 100000000 | bytes 5120768 | tf_op jit(solution)/shard_map/inner/pallas_call | solution.py:290
  13.9 0.0 collective-permute-done.low
  13.9 0.1 collective-permute-done.1.high
  14.1 0.0 copy-done.2
  14.1 2.1 %outer.1 = (bf16[16,64,128]{2,1,0:T(8,128)(2,1)}, f32[8,2,64,128]{3,2,1,0:T(8,128)S(1)}, f32[16,16,128]{2,1,0:T(8,128)S(1)}) custom-call(s32[32]{0:T(128)S(1)} %copy-done.5, s32[32]{0:T(128)S(1)} %copy-done.6, s32[4,32]{1,0:T(4,128)S(1)} %bitcast.10, f32[10,64,128]{2,1,0:T(8,128)S(1)} %collective-permute-done.low, ...), custom_call_target="tpu_custom_call" | custom-call | flops 100000000 | bytes 5382912 | tf_op jit(solution)/shard_map/outer/pallas_call | solution.py:290
  16.2 22.0 %all_to_all.15.sums = f32[16,16,128]{2,1,0:T(8,128)S(1)} all-to-all(f32[16,16,128]{2,1,0:T(8,128)S(1)} %get-tuple-element.21), channel_id=1, replica_groups=mesh['zh'=2,'y'=4,'x'=4,'slab'=16] {'slab'}, dimensions={0} | all-to-all | bytes 262144 | tf_op jit(solution)/shard_map/all_to_all | solution.py:373
  38.1 0.8 weigh.1
  38.9 24.8 %all_to_all.16.arrived = f32[16,128,128]{2,1,0:T(8,128)S(1)} all-to-all(f32[16,128,128]{2,1,0:T(8,128)S(1)} %get-tuple-element.23), channel_id=1, replica_groups=mesh['zh'=2,'y'=4,'x'=4,'slab'=16] {'y','x'}, dimensions={0} | all-to-all | bytes 2097152 | tf_op jit(solution)/shard_map/all_to_all | solution.py:384
  63.7 0.1 reduce.1.own
  63.7 8.2 %collective-permute-start.2 = (f32[136,128]{1,0:T(8,128)S(1)}, f32[136,128]{1,0:T(8,128)S(1)}, u32[]{:S(2)}, u32[]{:S(2)}) collective-permute-start(f32[136,128]{1,0:T(8,128)S(1)} %reduce.1.own), channel_id=1, source_target_pairs={{0,256},{256,0},{1,257},{257,1},{2,258},{258,2},{3,259},{259,3},{4... | collective-permute-start | bytes 208904 | tf_op jit(solution)/shard_map/ppermute | solution.py:388
  71.9 11.5 %collective-permute-done.2.other = f32[136,128]{1,0:T(8,128)S(1)} collective-permute-done((f32[136,128]{1,0:T(8,128)S(1)}, f32[136,128]{1,0:T(8,128)S(1)}, u32[]{:S(2)}, u32[]{:S(2)}) %collective-permute-start.2) | collective-permute-done | bytes 69664 | tf_op jit(solution)/shard_map/ppermute | solution.py:388
  83.4 0.1 spread.1
  83.5 20.6 %all_to_all.17.blocks = f32[16,136,128]{2,1,0:T(8,128)S(1)} all-to-all(f32[16,136,128]{2,1,0:T(8,128)S(1)} %spread.1), channel_id=1, replica_groups=mesh['zh'=2,'y'=4,'x'=4,'slab'=16] {'y','x'}, dimensions={0} | all-to-all | bytes 2228224 | tf_op jit(solution)/shard_map/all_to_all | solution.py:392
  104.0 1.4 %update.1 = f32[2,16,64,128]{3,2,1,0:T(8,128)} custom-call(f32[16,136,128]{2,1,0:T(8,128)S(1)} %all_to_all.17.blocks, f32[2,16,64,128]{3,2,1,0:T(8,128)S(1)} %copy-done), custom_call_target="tpu_custom_call" | custom-call | flops 1000000 | bytes 3211264 | tf_op jit(solution)/shard_map/update/pallas_call | solution.py:290
  (6 shorter events, 0.0 us)
Async XLA Ops:
  0.6 8.6 %copy-start.6 = (s32[32]{0:T(128)S(1)}, s32[32]{0:T(128)}, u32[]{:S(2)}) copy-start(s32[32]{0:T(128)} %counts.7) | copy-start | bytes 388
  0.6 8.6 %copy-start.5 = (s32[32]{0:T(128)S(1)}, s32[32]{0:T(128)}, u32[]{:S(2)}) copy-start(s32[32]{0:T(128)} %lengths.7) | copy-start | bytes 388
  0.7 8.6 %copy-start = (f32[2,16,64,128]{3,2,1,0:T(8,128)S(1)}, f32[2,16,64,128]{3,2,1,0:T(8,128)}, u32[]{:S(2)}) copy-start(f32[2,16,64,128]{3,2,1,0:T(8,128)} %fields.5) | copy-start | bytes 3145732
  0.7 8.6 %copy-start.4 = (s32[32,4]{0,1:T(4,128)S(1)}, s32[32,4]{0,1:T(4,128)}, u32[]{:S(2)}) copy-start(s32[32,4]{0,1:T(4,128)} %param.11) | copy-start | bytes 1540
  0.7 8.6 %copy-start.3 = (bf16[1,16,64,128]{3,2,1,0:T(8,128)(2,1)S(1)}, bf16[1,16,64,128]{3,2,1,0:T(8,128)(2,1)}, u32[]{:S(2)}) copy-start(bf16[1,16,64,128]{3,2,1,0:T(8,128)(2,1)} %param.6) | copy-start | bytes 786436
  3.6 10.3 %collective-permute-start = (f32[10,64,128]{2,1,0:T(8,128)}, f32[10,64,128]{2,1,0:T(8,128)S(1)}, u32[]{:S(2)}, u32[]{:S(2)}) collective-permute-start(f32[10,64,128]{2,1,0:T(8,128)} %get-tuple-element.14), channel_id=1, source_target_pairs={{0,1},{1,2},{2,3},{3,4},{4,5},{5,6},{6,7},{7,8},{8,9},{9,10},{10,1... | collective-permute-start | bytes 983048 | tf_op jit(solution)/shard_map/ppermute | solution.py:309
  5.5 8.5 %collective-permute-start.1 = (f32[10,64,128]{2,1,0:T(8,128)}, f32[10,64,128]{2,1,0:T(8,128)S(1)}, u32[]{:S(2)}, u32[]{:S(2)}) collective-permute-start(f32[10,64,128]{2,1,0:T(8,128)} %get-tuple-element.15), channel_id=1, source_target_pairs={{1,0},{2,1},{3,2},{4,3},{5,4},{6,5},{7,6},{8,7},{9,8},{10,9},{11,1... | collective-permute-start | bytes 983048 | tf_op jit(solution)/shard_map/ppermute | solution.py:309
  9.2 1.2 %copy-start.1 = (bf16[1,4,16,64,128]{4,3,2,1,0:T(8,128)(2,1)S(1)}, bf16[1,4,16,64,128]{4,3,2,1,0:T(8,128)(2,1)}, u32[]{:S(2)}) copy-start(bf16[1,4,16,64,128]{4,3,2,1,0:T(8,128)(2,1)} %param.7) | copy-start | bytes 3145732
  10.5 3.6 %copy-start.2 = (bf16[1,4,16,64,128]{4,3,2,1,0:T(8,128)(2,1)S(1)}, bf16[1,4,16,64,128]{4,3,2,1,0:T(8,128)(2,1)}, u32[]{:S(2)}) copy-start(bf16[1,4,16,64,128]{4,3,2,1,0:T(8,128)(2,1)} %param.7) | copy-start | bytes 3145732
  63.7 19.7 %collective-permute-start.2 = (f32[136,128]{1,0:T(8,128)S(1)}, f32[136,128]{1,0:T(8,128)S(1)}, u32[]{:S(2)}, u32[]{:S(2)}) collective-permute-start(f32[136,128]{1,0:T(8,128)S(1)} %reduce.1.own), channel_id=1, source_target_pairs={{0,256},{256,0},{1,257},{257,1},{2,258},{258,2},{3,259},{259,3},{4... | collective-permute-start | bytes 208904 | tf_op jit(solution)/shard_map/ppermute | solution.py:388

commit v3 on v2

--- a/solution.py
+++ b/solution.py
@@ -19,6 +19,7 @@
 
 VMEM = pl.BlockSpec(memory_space=pltpu.VMEM)
 SMEM = pl.BlockSpec(memory_space=pltpu.SMEM)
+UNROLL = True
 TOP = 8
 
 
@@ -134,7 +135,7 @@
                 w[later, p, rows, :] = half[kinds[s + 1], p] * fresh
             return carry
 
-        lax.fori_loop(s + 1, planes - 1 - s, each, 0, unroll=2)
+        lax.fori_loop(s + 1, planes - 1 - s, each, 0, unroll=UNROLL)
         if s == 0:
             sums[0] = total[...]
     sums[1] = total[...]
@@ -215,10 +216,10 @@
                 if s < rest:
                     w[side, later, r, rows, :] = half_of(side, r, kinds[s + 1]) * fresh
         if s == 0:
-            part = inner_sums[0] + total[...]
-            sums[:, 0:8] = jnp.broadcast_to(part[None], (sums.shape[0], 8, ny))
-    whole = inner_sums[1] + total[...]
-    sums[:, 8:16] = jnp.broadcast_to(whole[None], (sums.shape[0], 8, ny))
+            part = jnp.sum(inner_sums[0] + total[...], axis=0, keepdims=True)
+    whole = jnp.sum(inner_sums[1] + total[...], axis=0, keepdims=True)
+    both = jnp.concatenate([part, whole], 0)
+    sums[...] = jnp.broadcast_to(both[None], sums.shape)
     for p in range(planes - 2 * depth):
         final[depth + p] = middle[p]
 
@@ -233,9 +234,10 @@
         whole = whole + lengths[c]
     fraction = splat(lengths[cls].astype(jnp.float32)) / splat(whole.astype(jnp.float32))
     both = jnp.sum(sums[...], axis=0)
-    partition = jnp.sum(both[0:8]) / cells
+    partition = jnp.sum(both[0:1]) / cells
     weight = fraction * size / splat(partition)
-    extra[...] = weight * both[8:16]
+    first_row = lax.broadcasted_iota(jnp.int32, extra.shape, 0) == 0
+    extra[...] = jnp.where(first_row, weight * both[1:2], 0.0)
 
     def body(p, carry):
         for t in range(2):
@@ -358,7 +360,7 @@
         [
             jax.ShapeDtypeStruct((planes, nx, ny), jnp.bfloat16),
             f32(2 * depth, 2, nx, ny),
-            f32(slabs, 16, ny),
+            f32(slabs, 2, ny),
         ],
         [
             pltpu.VMEM((2, 2, 2 * depth + 2, padded, ny), jnp.float32),

time: 106 us -> 104 us (0.981)
  Pallas kernels: 10.7 us -> 9.17 us
    ppermute x1, waiting for transfers between devices: 11.5 us -> 9.67 us  [body(): other = lax.ppermute(own, 'zh', [(0, 1), (1, 0)])]
    pallas_call x7, Pallas kernels: 10.7 us -> 9.17 us  [call(): pl.pallas_call(kernel, out_shape=outs, in_specs=[SMEM] * smem + [VMEM] *...]
    ppermute x2, waiting for transfers between devices: 0.13 us -> 1.69 us  [swapped(): return lax.ppermute(x, axis, pairs)]
  transfers between devices with their start and end apart: 3 -> 3, of which waited for: 2 -> 2; matrix products, arithmetic and copies ran while one was open for 0% -> 0% of each run, Pallas kernels for 3% -> 2%
where the time goes in v3:
time: 104 us
  blocking collectives  67.5 us (65%)
  starting transfers between devices  13.8 us (13%)
  waiting for transfers between devices  11.4 us (11%)
  Pallas kernels  9.17 us (9%)
  local copies, waits for them, and re-layouts  1.24 us (1%)
    all_to_all x1, blocking collectives, body(): arrived = lax.all_to_all(sent, XY, 0, 0, tiled=True)  24.3 us
    all_to_all x1, blocking collectives, body(): sums = lax.all_to_all(sums, SLAB, 0, 0, tiled=True)  21.7 us
    all_to_all x1, blocking collectives, body(): blocks = lax.all_to_all(blocks, XY, 0, 0, tiled=True)  21.6 us
    ppermute x1, waiting for transfers between devices, body(): other = lax.ppermute(own, 'zh', [(0, 1), (1, 0)])  9.67 us
    pallas_call x7, Pallas kernels, call(): pl.pallas_call(kernel, out_shape=outs, in_specs=[SMEM] * smem + [VMEM] *...  9.17 us
    ppermute x1, starting transfers between devices, body(): other = lax.ppermute(own, 'zh', [(0, 1), (1, 0)])  8.22 us
    ppermute x2, starting transfers between devices, swapped(): return lax.ppermute(x, axis, pairs)  5.56 us
  transfers between devices with their start and end apart: 3, of which 2 were waited for; matrix products, arithmetic and copies ran while one was open for 0% of the time, Pallas kernels for 2%

profile of v3, /device:TPU:32, one launch (start us, length us, event | category | flops | bytes accessed | tf_op | source)
XLA Modules:
  0.0 103.9 jit_solution(18067241318761149133)
XLA Ops:
  0.6 0.0 copy-start.6
  0.6 0.0 copy-start.5
  0.7 0.0 copy-start
  0.7 0.0 copy-start.4
  0.7 0.0 copy-start.3
  0.7 2.9 %edges.1 = (f32[10,64,128]{2,1,0:T(8,128)}, f32[10,64,128]{2,1,0:T(8,128)}) custom-call(s32[32]{0:T(128)} %lengths.7, s32[32]{0:T(128)} %counts.7, s32[4,32]{1,0:T(4,128)} %bitcast.8, bf16[16,64,128]{2,1,0:T(8,128)(2,1)} %bitcast.6, f32[2,16,64,128]{3,2,1,0:T(8,128)} %fields.5), custom_call_target="tpu_custom_call" | custom-call | flops 1000000 | bytes 1966848 | tf_op jit(solution)/shard_map/edges/pallas_call | solution.py:292
  3.6 1.9 %collective-permute-start = (f32[10,64,128]{2,1,0:T(8,128)}, f32[10,64,128]{2,1,0:T(8,128)S(1)}, u32[]{:S(2)}, u32[]{:S(2)}) collective-permute-start(f32[10,64,128]{2,1,0:T(8,128)} %get-tuple-element.14), channel_id=1, source_target_pairs={{0,1},{1,2},{2,3},{3,4},{4,5},{5,6},{6,7},{7,8},{8,9},{9,10},{10,1... | collective-permute-start | bytes 983048 | tf_op jit(solution)/shard_map/ppermute | solution.py:311
  5.5 3.6 %collective-permute-start.1 = (f32[10,64,128]{2,1,0:T(8,128)}, f32[10,64,128]{2,1,0:T(8,128)S(1)}, u32[]{:S(2)}, u32[]{:S(2)}) collective-permute-start(f32[10,64,128]{2,1,0:T(8,128)} %get-tuple-element.15), channel_id=1, source_target_pairs={{1,0},{2,1},{3,2},{4,3},{5,4},{6,5},{7,6},{8,7},{9,8},{10,9},{11,1... | collective-permute-start | bytes 983048 | tf_op jit(solution)/shard_map/ppermute | solution.py:311
  9.2 0.0 copy-start.1
  9.2 1.2 %copy-done.1 = bf16[1,4,16,64,128]{4,3,2,1,0:T(8,128)(2,1)S(1)} copy-done((bf16[1,4,16,64,128]{4,3,2,1,0:T(8,128)(2,1)S(1)}, bf16[1,4,16,64,128]{4,3,2,1,0:T(8,128)(2,1)}, u32[]{:S(2)}) %copy-start.1) | copy-done | bytes 1048600
  10.5 1.9 %inner.1 = (f32[2,16,64,128]{3,2,1,0:T(8,128)S(1)}, f32[4,4,64,128]{3,2,1,0:T(8,128)S(1)}, f32[16,2,64,128]{3,2,1,0:T(8,128)S(1)}, bf16[8,64,128]{2,1,0:T(8,128)(2,1)S(1)}, f32[2,8,128]{2,1,0:T(8,128)S(1)}) custom-call(s32[32]{0:T(128)S(1)} %copy-done.5, s32[32]{0:T(128)S(1)} %copy-done.6, s32[4,32]{1,0:T(4,128)S(1)} %bitcast.9, ...), custom_call_target="tpu_custom_call" | custom-call | flops 100000000 | bytes 5120768 | tf_op jit(solution)/shard_map/inner/pallas_call | solution.py:292
  12.4 0.0 collective-permute-done.low
  12.4 1.7 %collective-permute-done.1.high = f32[10,64,128]{2,1,0:T(8,128)S(1)} collective-permute-done((f32[10,64,128]{2,1,0:T(8,128)}, f32[10,64,128]{2,1,0:T(8,128)S(1)}, u32[]{:S(2)}, u32[]{:S(2)}) %collective-permute-start.1) | collective-permute-done | bytes 327712 | tf_op jit(solution)/shard_map/ppermute | solution.py:311
  14.1 0.0 copy-done.2
  14.1 2.1 %outer.1 = (bf16[16,64,128]{2,1,0:T(8,128)(2,1)}, f32[8,2,64,128]{3,2,1,0:T(8,128)S(1)}, f32[16,2,128]{2,1,0:T(2,128)S(1)}) custom-call(s32[32]{0:T(128)S(1)} %copy-done.5, s32[32]{0:T(128)S(1)} %copy-done.6, s32[4,32]{1,0:T(4,128)S(1)} %bitcast.10, f32[10,64,128]{2,1,0:T(8,128)S(1)} %collective-permute-done.low, ...), custom_call_target="tpu_custom_call" | custom-call | flops 100000000 | bytes 5268224 | tf_op jit(solution)/shard_map/outer/pallas_call | solution.py:292
  16.2 21.7 %all_to_all.15.sums = f32[16,2,128]{2,1,0:T(2,128)S(1)} all-to-all(f32[16,2,128]{2,1,0:T(2,128)S(1)} %get-tuple-element.21), channel_id=1, replica_groups=mesh['zh'=2,'y'=4,'x'=4,'slab'=16] {'slab'}, dimensions={0} | all-to-all | bytes 32768 | tf_op jit(solution)/shard_map/all_to_all | solution.py:375
  37.9 0.8 weigh.1
  38.6 24.3 %all_to_all.16.arrived = f32[16,128,128]{2,1,0:T(8,128)S(1)} all-to-all(f32[16,128,128]{2,1,0:T(8,128)S(1)} %get-tuple-element.23), channel_id=1, replica_groups=mesh['zh'=2,'y'=4,'x'=4,'slab'=16] {'y','x'}, dimensions={0} | all-to-all | bytes 2097152 | tf_op jit(solution)/shard_map/all_to_all | solution.py:386
  62.9 0.1 reduce.1.own
  63.0 8.2 %collective-permute-start.2 = (f32[136,128]{1,0:T(8,128)S(1)}, f32[136,128]{1,0:T(8,128)S(1)}, u32[]{:S(2)}, u32[]{:S(2)}) collective-permute-start(f32[136,128]{1,0:T(8,128)S(1)} %reduce.1.own), channel_id=1, source_target_pairs={{0,256},{256,0},{1,257},{257,1},{2,258},{258,2},{3,259},{259,3},{4... | collective-permute-start | bytes 208904 | tf_op jit(solution)/shard_map/ppermute | solution.py:390
  71.2 9.7 %collective-permute-done.2.other = f32[136,128]{1,0:T(8,128)S(1)} collective-permute-done((f32[136,128]{1,0:T(8,128)S(1)}, f32[136,128]{1,0:T(8,128)S(1)}, u32[]{:S(2)}, u32[]{:S(2)}) %collective-permute-start.2) | collective-permute-done | bytes 69664 | tf_op jit(solution)/shard_map/ppermute | solution.py:390
  80.9 0.1 spread.1
  80.9 21.6 %all_to_all.17.blocks = f32[16,136,128]{2,1,0:T(8,128)S(1)} all-to-all(f32[16,136,128]{2,1,0:T(8,128)S(1)} %spread.1), channel_id=1, replica_groups=mesh['zh'=2,'y'=4,'x'=4,'slab'=16] {'y','x'}, dimensions={0} | all-to-all | bytes 2228224 | tf_op jit(solution)/shard_map/all_to_all | solution.py:394
  102.5 1.4 %update.1 = f32[2,16,64,128]{3,2,1,0:T(8,128)} custom-call(f32[16,136,128]{2,1,0:T(8,128)S(1)} %all_to_all.17.blocks, f32[2,16,64,128]{3,2,1,0:T(8,128)S(1)} %copy-done), custom_call_target="tpu_custom_call" | custom-call | flops 1000000 | bytes 3211264 | tf_op jit(solution)/shard_map/update/pallas_call | solution.py:292
  (6 shorter events, 0.0 us)
Async XLA Ops:
  0.6 8.6 %copy-start.6 = (s32[32]{0:T(128)S(1)}, s32[32]{0:T(128)}, u32[]{:S(2)}) copy-start(s32[32]{0:T(128)} %counts.7) | copy-start | bytes 388
  0.6 8.6 %copy-start.5 = (s32[32]{0:T(128)S(1)}, s32[32]{0:T(128)}, u32[]{:S(2)}) copy-start(s32[32]{0:T(128)} %lengths.7) | copy-start | bytes 388
  0.7 8.6 %copy-start = (f32[2,16,64,128]{3,2,1,0:T(8,128)S(1)}, f32[2,16,64,128]{3,2,1,0:T(8,128)}, u32[]{:S(2)}) copy-start(f32[2,16,64,128]{3,2,1,0:T(8,128)} %fields.5) | copy-start | bytes 3145732
  0.7 8.6 %copy-start.4 = (s32[32,4]{0,1:T(4,128)S(1)}, s32[32,4]{0,1:T(4,128)}, u32[]{:S(2)}) copy-start(s32[32,4]{0,1:T(4,128)} %param.11) | copy-start | bytes 1540
  0.7 8.6 %copy-start.3 = (bf16[1,16,64,128]{3,2,1,0:T(8,128)(2,1)S(1)}, bf16[1,16,64,128]{3,2,1,0:T(8,128)(2,1)}, u32[]{:S(2)}) copy-start(bf16[1,16,64,128]{3,2,1,0:T(8,128)(2,1)} %param.6) | copy-start | bytes 786436
  3.6 8.8 %collective-permute-start = (f32[10,64,128]{2,1,0:T(8,128)}, f32[10,64,128]{2,1,0:T(8,128)S(1)}, u32[]{:S(2)}, u32[]{:S(2)}) collective-permute-start(f32[10,64,128]{2,1,0:T(8,128)} %get-tuple-element.14), channel_id=1, source_target_pairs={{0,1},{1,2},{2,3},{3,4},{4,5},{5,6},{6,7},{7,8},{8,9},{9,10},{10,1... | collective-permute-start | bytes 983048 | tf_op jit(solution)/shard_map/ppermute | solution.py:311
  5.5 8.5 %collective-permute-start.1 = (f32[10,64,128]{2,1,0:T(8,128)}, f32[10,64,128]{2,1,0:T(8,128)S(1)}, u32[]{:S(2)}, u32[]{:S(2)}) collective-permute-start(f32[10,64,128]{2,1,0:T(8,128)} %get-tuple-element.15), channel_id=1, source_target_pairs={{1,0},{2,1},{3,2},{4,3},{5,4},{6,5},{7,6},{8,7},{9,8},{10,9},{11,1... | collective-permute-start | bytes 983048 | tf_op jit(solution)/shard_map/ppermute | solution.py:311
  9.2 1.2 %copy-start.1 = (bf16[1,4,16,64,128]{4,3,2,1,0:T(8,128)(2,1)S(1)}, bf16[1,4,16,64,128]{4,3,2,1,0:T(8,128)(2,1)}, u32[]{:S(2)}) copy-start(bf16[1,4,16,64,128]{4,3,2,1,0:T(8,128)(2,1)} %param.7) | copy-start | bytes 3145732
  10.5 3.6 %copy-start.2 = (bf16[1,4,16,64,128]{4,3,2,1,0:T(8,128)(2,1)S(1)}, bf16[1,4,16,64,128]{4,3,2,1,0:T(8,128)(2,1)}, u32[]{:S(2)}) copy-start(bf16[1,4,16,64,128]{4,3,2,1,0:T(8,128)(2,1)} %param.7) | copy-start | bytes 3145732
  63.0 17.9 %collective-permute-start.2 = (f32[136,128]{1,0:T(8,128)S(1)}, f32[136,128]{1,0:T(8,128)S(1)}, u32[]{:S(2)}, u32[]{:S(2)}) collective-permute-start(f32[136,128]{1,0:T(8,128)S(1)} %reduce.1.own), channel_id=1, source_target_pairs={{0,256},{256,0},{1,257},{257,1},{2,258},{258,2},{3,259},{259,3},{4... | collective-permute-start | bytes 208904 | tf_op jit(solution)/shard_map/ppermute | solution.py:390

commit v4 on v3

--- a/solution.py
+++ b/solution.py
@@ -61,33 +61,40 @@
     w[:, :, TOP + nx : TOP + nx + TOP, :] = blank
 
 
-def edges_kernel(lengths, counts, types, q, fields, up, down, ends, sems):
+def sides():
+    core = lax.rem(lax.axis_index(SLAB), 2)
+    return core, 1 - core
+
+
+def edges_kernel(lengths, counts, types, q, fields, outward, inward, ends, sems):
     planes = q.shape[0]
     depth = types.shape[0]
     cls = own_class()
     kind = types[0, cls]
     rest = depth - 1
+    messages = (outward, inward)
     copies = []
-    for side, start in enumerate((planes - depth, 0)):
-        copies.append((q.at[pl.ds(start, depth)], ends.at[side]))
-    for t in range(2):
-        at = pl.ds(depth + t * rest, rest)
-        copies.append((fields.at[t, pl.ds(planes - rest, rest)], up.at[at]))
-        copies.append((fields.at[t, pl.ds(0, rest)], down.at[at]))
-    copies.append((fields.at[kind, pl.ds(planes - depth, 1)], up.at[pl.ds(0, 1)]))
-    copies.append((fields.at[kind, pl.ds(rest, 1)], down.at[pl.ds(rest, 1)]))
+    for m, upper in enumerate(sides()):
+        start, turn = upper * (planes - depth) + (1 - upper) * rest, 2 * upper - 1
+        for r in range(depth):
+            at = start + turn * r
+            copies.append((q.at[at], ends.at[m, r]))
+            if r == 0:
+                copies.append((fields.at[kind, at], messages[m].at[0]))
+            else:
+                for t in range(2):
+                    copies.append((fields.at[t, at], messages[m].at[depth + t * rest + r - 1]))
     copies = [pltpu.make_async_copy(a, b, sems.at[i]) for i, (a, b) in enumerate(copies)]
     for copy in copies:
         copy.start()
+    scale = -0.5 * size_of(lengths, counts, cls)
     for copy in copies:
         copy.wait()
-    scale = -0.5 * size_of(lengths, counts, cls)
     ours = depth + kind * rest
-    for p in range(depth):
-        chosen = up[0] if p == 0 else up[ours + p - 1]
-        up[p] = jnp.exp(scale * chosen) * ends[0, p].astype(jnp.float32)
-        chosen = down[rest] if p == rest else down[ours + p]
-        down[p] = jnp.exp(scale * chosen) * ends[1, p].astype(jnp.float32)
+    for m, message in enumerate(messages):
+        for r in range(depth):
+            chosen = message[0] if r == 0 else message[ours + r - 1]
+            message[r] = jnp.exp(scale * chosen) * ends[m, r].astype(jnp.float32)
 
 
 def inner_kernel(
@@ -145,8 +152,8 @@
     lengths,
     counts,
     types,
-    low,
-    high,
+    outer,
+    near,
     back,
     half,
     state,
@@ -163,10 +170,8 @@
     depth = back.shape[0]
     cls = own_class()
     slab = lax.axis_index(SLAB)
-    inside = (
-        splat(jnp.where(slab > 0, 1.0, 0.0)),
-        splat(jnp.where(slab < lax.axis_size(SLAB) - 1, 1.0, 0.0)),
-    )
+    inside = jnp.logical_and(slab > 0, slab < lax.axis_size(SLAB) - 1)
+    inside = splat(jnp.where(inside, 1.0, 0.0))
     size = size_of(lengths, counts, cls)
     spread = diffusion_scale * size
     keep = 1.0 - 6.0 * spread
@@ -177,44 +182,46 @@
         clear_margins(w.at[side], nx)
     total[...] = jnp.zeros_like(total)
     rows = slice(TOP, TOP + nx)
-    came = (low, high)
+    came = (outer, near)
     rest = depth - 1
-
-    def half_of(side, r, kind):
+    upper = sides()
+
+    def place(m, r):
+        return upper[m] * (planes - 1) + (1 - 2 * upper[m]) * (r - depth)
+
+    def half_of(m, r, kind):
         if r >= depth:
-            return half[kind, r - depth if side == 0 else planes - 1 + depth - r]
-        at = r - 1 if side == 0 else rest - r
-        return jnp.exp(scale * came[side][depth + kind * rest + at])
-
-    for side in range(2):
+            return half[kind, place(m, r)]
+        return jnp.exp(scale * came[m][depth + kind * rest + r - 1])
+
+    for m in range(2):
         for r in range(depth):
-            w[side, 0, r, rows, :] = came[side][r if side == 0 else rest - r]
+            w[m, 0, r, rows, :] = came[m][r]
         for p in range(depth):
-            at = p if side == 0 else planes - 1 - p
             for t in range(2):
-                edge_dens[side * depth + p, t] = dens[at, t]
+                edge_dens[upper[m] * depth + p, t] = dens[place(m, depth + p), t]
 
     for s in range(depth):
         now, later = s % 2, (s + 1) % 2
-        for side in range(2):
+        for m in range(2):
             for i in range(2):
-                w[side, now, s + depth + i, rows, :] = state[s, 2 * side + i]
+                w[m, now, s + depth + i, rows, :] = state[s, 2 * upper[m] + i]
         for i in range(depth):
-            for side in range(2):
+            for m in range(2):
                 r = s + 1 + i
-                core, beside = neighbours(w, (side, now), r, edge_low, edge_high, nx)
-                fresh = half_of(side, r, kinds[s]) * (keep * core + spread * beside)
-                if r < depth:
-                    fresh = inside[side] * fresh
-                else:
-                    at = r - depth if side == 0 else planes - 1 + depth - r
+                core, beside = neighbours(w, (m, now), r, edge_low, edge_high, nx)
+                fresh = half_of(m, r, kinds[s]) * (keep * core + spread * beside)
+                if r >= depth:
+                    at = place(m, r)
                     product = fresh * back[s, at].astype(jnp.float32)
-                    edge_dens[side * depth + r - depth, kinds[s]] += product
+                    edge_dens[upper[m] * depth + r - depth, kinds[s]] += product
                     total[...] += folded(product)
                     if s == rest:
                         final[at] = fresh.astype(jnp.bfloat16)
+                elif m == 0:
+                    fresh = inside * fresh
                 if s < rest:
-                    w[side, later, r, rows, :] = half_of(side, r, kinds[s + 1]) * fresh
+                    w[m, later, r, rows, :] = half_of(m, r, kinds[s + 1]) * fresh
         if s == 0:
             part = jnp.sum(inner_sums[0] + total[...], axis=0, keepdims=True)
     whole = jnp.sum(inner_sums[1] + total[...], axis=0, keepdims=True)
@@ -263,8 +270,8 @@
     out[acc.shape[0] :] = extra[...]
 
 
-def spread_kernel(own, other, blocks):
-    both = own[...] + other[...]
+def spread_kernel(pair, blocks):
+    both = pair[0] + pair[1]
     blocks[...] = jnp.broadcast_to(both[None], blocks.shape)
 
 
@@ -305,12 +312,6 @@
     return jax.ShapeDtypeStruct(shape, jnp.float32)
 
 
-def swapped(x, axis, shift):
-    count = lax.axis_size(axis)
-    pairs = [(i, i + shift) for i in range(count) if 0 <= i + shift < count]
-    return lax.ppermute(x, axis, pairs)
-
-
 def body(q_init, q_back, fields, lengths, counts, types):
     _, planes, nx, ny = q_init.shape
     depth = q_back.shape[1]
@@ -321,10 +322,10 @@
     slabs = lax.axis_size(SLAB)
     message = f32(3 * depth - 2, nx, ny)
 
-    up, down = call(
+    outward, inward = call(
         edges_kernel,
         [message, message],
-        [pltpu.VMEM((2, depth, nx, ny), jnp.bfloat16), pltpu.SemaphoreType.DMA((8,))],
+        [pltpu.VMEM((2, depth, nx, ny), jnp.bfloat16), pltpu.SemaphoreType.DMA((2 * (3 * depth - 1),))],
         (lengths, counts, types, q, fields),
         3,
         10**6,
@@ -332,8 +333,10 @@
         vmem=None,
         hbm=2,
     )
-    low = swapped(up, SLAB, 1)
-    high = swapped(down, SLAB, -1)
+    across = [(i, i + 1) for i in range(1, slabs - 1, 2)]
+    within = [(i, i + 1) for i in range(0, slabs, 2)]
+    outer = lax.ppermute(outward, SLAB, across + [(b, a) for a, b in across])
+    near = lax.ppermute(inward, SLAB, within + [(b, a) for a, b in within])
 
     padded = nx + 2 * TOP
     half, state, dens, middle, sums = call(
@@ -366,7 +369,7 @@
             pltpu.VMEM((2, 2, 2 * depth + 2, padded, ny), jnp.float32),
             pltpu.VMEM((8, ny), jnp.float32),
         ],
-        (lengths, counts, types, low, high, back, half, state, dens, middle, sums),
+        (lengths, counts, types, outer, near, back, half, state, dens, middle, sums),
         3,
         10**8,
         "outer",
@@ -387,9 +390,9 @@
     (own,) = call(
         reduce_kernel, [f32(2 * nx + 8, ny)], [], (arrived, extra), 0, 10**6, "reduce", vmem=8
     )
-    other = lax.ppermute(own, "zh", [(0, 1), (1, 0)])
+    pair = lax.all_gather(own, "zh", axis=0, tiled=False)
     (blocks,) = call(
-        spread_kernel, [f32(peers, 2 * nx + 8, ny)], [], (own, other), 0, 10**6, "spread", vmem=8
+        spread_kernel, [f32(peers, 2 * nx + 8, ny)], [], (pair,), 0, 10**6, "spread", vmem=8
     )
     blocks = lax.all_to_all(blocks, XY, 0, 0, tiled=True)
     (fields_new,) = call(

time: 104 us -> 101 us (0.971)
  blocking collectives: 67.5 us -> 83.4 us
  waiting for transfers between devices: 11.4 us -> 0.01 us
  starting transfers between devices: 13.8 us -> 5.85 us
    all_gather x0 -> x1, blocking collectives: none -> 16.7 us  [body(): pair = lax.all_gather(own, 'zh', axis=0, tiled=False)]
    ppermute x3 -> x2, waiting for transfers between devices: 11.4 us -> 0.01 us  [the longest x1 0.01 us: body(): outer = lax.ppermute(outward, SLAB, across + [(b, a) for a, b in across])]
    ppermute x3 -> x2, starting transfers between devices: 13.8 us -> 5.85 us  [the longest x1 3.93 us: body(): near = lax.ppermute(inward, SLAB, within + [(b, a) for a, b in within])]
  transfers between devices with their start and end apart: 3 -> 2, of which waited for: 2 -> 0; matrix products, arithmetic and copies ran while one was open for 0% -> 0% of each run, Pallas kernels for 2% -> 2%
where the time goes in v4:
time: 101 us
  blocking collectives  83.4 us (83%)
  Pallas kernels  9.28 us (9%)
  starting transfers between devices  5.85 us (6%)
  local copies, waits for them, and re-layouts  1.24 us (1%)
    all_to_all x1, blocking collectives, body(): arrived = lax.all_to_all(sent, XY, 0, 0, tiled=True)  24.3 us
    all_to_all x1, blocking collectives, body(): blocks = lax.all_to_all(blocks, XY, 0, 0, tiled=True)  21.6 us
    all_to_all x1, blocking collectives, body(): sums = lax.all_to_all(sums, SLAB, 0, 0, tiled=True)  20.8 us
    all_gather x1, blocking collectives, body(): pair = lax.all_gather(own, 'zh', axis=0, tiled=False)  16.7 us
    pallas_call x7, Pallas kernels, call(): pl.pallas_call(kernel, out_shape=outs, in_specs=[SMEM] * smem + [VMEM] *...  9.28 us
    ppermute x1, starting transfers between devices, body(): near = lax.ppermute(inward, SLAB, within + [(b, a) for a, b in within])  3.93 us
  transfers between devices with their start and end apart: 2, of which 0 were waited for; matrix products, arithmetic and copies ran while one was open for 0% of the time, Pallas kernels for 2%

profile of v4, /device:TPU:32, one launch (start us, length us, event | category | flops | bytes accessed | tf_op | source)
XLA Modules:
  0.0 100.5 jit_solution(17788451317982509784)
XLA Ops:
  0.6 0.0 copy-start.6
  0.6 0.0 copy-start.5
  0.7 0.0 copy-start
  0.7 0.0 copy-start.4
  0.7 0.0 copy-start.3
  0.7 3.0 %edges.1 = (f32[10,64,128]{2,1,0:T(8,128)}, f32[10,64,128]{2,1,0:T(8,128)}) custom-call(s32[32]{0:T(128)} %lengths.7, s32[32]{0:T(128)} %counts.7, s32[4,32]{1,0:T(4,128)} %bitcast.10, bf16[16,64,128]{2,1,0:T(8,128)(2,1)} %bitcast.7, f32[2,16,64,128]{3,2,1,0:T(8,128)} %fields.5), custom_call_target="tpu_custom_call" | custom-call | flops 1000000 | bytes 1966848 | tf_op jit(solution)/shard_map/edges/pallas_call | solution.py:299
  3.7 1.9 %collective-permute-start = (f32[10,64,128]{2,1,0:T(8,128)}, f32[10,64,128]{2,1,0:T(8,128)S(1)}, u32[]{:S(2)}, u32[]{:S(2)}) collective-permute-start(f32[10,64,128]{2,1,0:T(8,128)} %get-tuple-element.14), channel_id=1, source_target_pairs={{1,2},{3,4},{5,6},{7,8},{9,10},{11,12},{13,14},{2,1},{4,3},{6,5},{... | collective-permute-start | bytes 983048 | tf_op jit(solution)/shard_map/ppermute | solution.py:338
  5.6 3.9 %collective-permute-start.1 = (f32[10,64,128]{2,1,0:T(8,128)}, f32[10,64,128]{2,1,0:T(8,128)S(1)}, u32[]{:S(2)}, u32[]{:S(2)}) collective-permute-start(f32[10,64,128]{2,1,0:T(8,128)} %get-tuple-element.15), channel_id=1, source_target_pairs={{0,1},{2,3},{4,5},{6,7},{8,9},{10,11},{12,13},{14,15},{1,0},{3,2},... | collective-permute-start | bytes 983048 | tf_op jit(solution)/shard_map/ppermute | solution.py:339
  9.5 0.0 copy-done.6
  9.5 0.0 copy-done.5
  9.6 0.0 copy-start.1
  9.6 1.2 %copy-done.1 = bf16[1,4,16,64,128]{4,3,2,1,0:T(8,128)(2,1)S(1)} copy-done((bf16[1,4,16,64,128]{4,3,2,1,0:T(8,128)(2,1)S(1)}, bf16[1,4,16,64,128]{4,3,2,1,0:T(8,128)(2,1)}, u32[]{:S(2)}) %copy-start.1) | copy-done | bytes 1048600
  10.8 1.9 %inner.1 = (f32[2,16,64,128]{3,2,1,0:T(8,128)S(1)}, f32[4,4,64,128]{3,2,1,0:T(8,128)S(1)}, f32[16,2,64,128]{3,2,1,0:T(8,128)S(1)}, bf16[8,64,128]{2,1,0:T(8,128)(2,1)S(1)}, f32[2,8,128]{2,1,0:T(8,128)S(1)}) custom-call(s32[32]{0:T(128)S(1)} %copy-done.5, s32[32]{0:T(128)S(1)} %copy-done.6, s32[4,32]{1,0:T(4,128)S(1)} %bitcast.11, ...), custom_call_target="tpu_custom_call" | custom-call | flops 100000000 | bytes 5120768 | tf_op jit(solution)/shard_map/inner/pallas_call | solution.py:299
  12.8 0.0 collective-permute-done.outer
  12.8 0.0 collective-permute-done.1.near
  12.8 2.1 %outer.1 = (bf16[16,64,128]{2,1,0:T(8,128)(2,1)}, f32[8,2,64,128]{3,2,1,0:T(8,128)S(1)}, f32[16,2,128]{2,1,0:T(2,128)S(1)}) custom-call(s32[32]{0:T(128)S(1)} %copy-done.5, s32[32]{0:T(128)S(1)} %copy-done.6, s32[4,32]{1,0:T(4,128)S(1)} %bitcast.12, f32[10,64,128]{2,1,0:T(8,128)S(1)} %collective-permute-done.outer, ...), custom_call_target="tpu_custom_call" | custom-call | flops 100000000 | bytes 5268224 | tf_op jit(solution)/shard_map/outer/pallas_call | solution.py:299
  14.9 20.8 %all_to_all.15.sums = f32[16,2,128]{2,1,0:T(2,128)S(1)} all-to-all(f32[16,2,128]{2,1,0:T(2,128)S(1)} %get-tuple-element.21), channel_id=1, replica_groups=mesh['zh'=2,'y'=4,'x'=4,'slab'=16] {'slab'}, dimensions={0} | all-to-all | bytes 32768 | tf_op jit(solution)/shard_map/all_to_all | solution.py:378
  35.7 0.8 weigh.1
  36.5 24.3 %all_to_all.16.arrived = f32[16,128,128]{2,1,0:T(8,128)S(1)} all-to-all(f32[16,128,128]{2,1,0:T(8,128)S(1)} %get-tuple-element.23), channel_id=1, replica_groups=mesh['zh'=2,'y'=4,'x'=4,'slab'=16] {'y','x'}, dimensions={0} | all-to-all | bytes 2097152 | tf_op jit(solution)/shard_map/all_to_all | solution.py:389
  60.8 0.1 reduce.1
  60.8 16.7 %all-gather = f32[272,128]{1,0:T(8,128)S(1)} all-gather(f32[136,128]{1,0:T(8,128)S(1)} %reduce.1), channel_id=2, replica_groups=mesh['zh'=2,'y'=4,'x'=4,'slab'=16] {'zh'}, dimensions={0}, use_global_device_ids=true | all-gather | bytes 208896 | tf_op jit(solution)/shard_map/all_gather | solution.py:393
  77.5 0.1 spread.1
  77.6 21.6 %all_to_all.17.blocks = f32[16,136,128]{2,1,0:T(8,128)S(1)} all-to-all(f32[16,136,128]{2,1,0:T(8,128)S(1)} %spread.1), channel_id=1, replica_groups=mesh['zh'=2,'y'=4,'x'=4,'slab'=16] {'y','x'}, dimensions={0} | all-to-all | bytes 2228224 | tf_op jit(solution)/shard_map/all_to_all | solution.py:397
  99.2 1.4 %update.1 = f32[2,16,64,128]{3,2,1,0:T(8,128)} custom-call(f32[16,136,128]{2,1,0:T(8,128)S(1)} %all_to_all.17.blocks, f32[2,16,64,128]{3,2,1,0:T(8,128)S(1)} %copy-done), custom_call_target="tpu_custom_call" | custom-call | flops 1000000 | bytes 3211264 | tf_op jit(solution)/shard_map/update/pallas_call | solution.py:299
  (5 shorter events, 0.0 us)
Async XLA Ops:
  0.6 8.9 %copy-start.6 = (s32[32]{0:T(128)S(1)}, s32[32]{0:T(128)}, u32[]{:S(2)}) copy-start(s32[32]{0:T(128)} %counts.7) | copy-start | bytes 388
  0.6 8.9 %copy-start.5 = (s32[32]{0:T(128)S(1)}, s32[32]{0:T(128)}, u32[]{:S(2)}) copy-start(s32[32]{0:T(128)} %lengths.7) | copy-start | bytes 388
  0.7 8.9 %copy-start = (f32[2,16,64,128]{3,2,1,0:T(8,128)S(1)}, f32[2,16,64,128]{3,2,1,0:T(8,128)}, u32[]{:S(2)}) copy-start(f32[2,16,64,128]{3,2,1,0:T(8,128)} %fields.5) | copy-start | bytes 3145732
  0.7 8.9 %copy-start.4 = (s32[32,4]{0,1:T(4,128)S(1)}, s32[32,4]{0,1:T(4,128)}, u32[]{:S(2)}) copy-start(s32[32,4]{0,1:T(4,128)} %param.11) | copy-start | bytes 1540
  0.7 8.9 %copy-start.3 = (bf16[1,16,64,128]{3,2,1,0:T(8,128)(2,1)S(1)}, bf16[1,16,64,128]{3,2,1,0:T(8,128)(2,1)}, u32[]{:S(2)}) copy-start(bf16[1,16,64,128]{3,2,1,0:T(8,128)(2,1)} %param.6) | copy-start | bytes 786436
  3.7 9.1 %collective-permute-start = (f32[10,64,128]{2,1,0:T(8,128)}, f32[10,64,128]{2,1,0:T(8,128)S(1)}, u32[]{:S(2)}, u32[]{:S(2)}) collective-permute-start(f32[10,64,128]{2,1,0:T(8,128)} %get-tuple-element.14), channel_id=1, source_target_pairs={{1,2},{3,4},{5,6},{7,8},{9,10},{11,12},{13,14},{2,1},{4,3},{6,5},{... | collective-permute-start | bytes 983048 | tf_op jit(solution)/shard_map/ppermute | solution.py:338
  5.6 7.2 %collective-permute-start.1 = (f32[10,64,128]{2,1,0:T(8,128)}, f32[10,64,128]{2,1,0:T(8,128)S(1)}, u32[]{:S(2)}, u32[]{:S(2)}) collective-permute-start(f32[10,64,128]{2,1,0:T(8,128)} %get-tuple-element.15), channel_id=1, source_target_pairs={{0,1},{2,3},{4,5},{6,7},{8,9},{10,11},{12,13},{14,15},{1,0},{3,2},... | collective-permute-start | bytes 983048 | tf_op jit(solution)/shard_map/ppermute | solution.py:339
  9.6 1.2 %copy-start.1 = (bf16[1,4,16,64,128]{4,3,2,1,0:T(8,128)(2,1)S(1)}, bf16[1,4,16,64,128]{4,3,2,1,0:T(8,128)(2,1)}, u32[]{:S(2)}) copy-start(bf16[1,4,16,64,128]{4,3,2,1,0:T(8,128)(2,1)} %param.7) | copy-start | bytes 3145732
  10.8 2.0 %copy-start.2 = (bf16[1,4,16,64,128]{4,3,2,1,0:T(8,128)(2,1)S(1)}, bf16[1,4,16,64,128]{4,3,2,1,0:T(8,128)(2,1)}, u32[]{:S(2)}) copy-start(bf16[1,4,16,64,128]{4,3,2,1,0:T(8,128)(2,1)} %param.7) | copy-start | bytes 3145732

commit v5 on v4

--- a/solution.py
+++ b/solution.py
@@ -29,10 +29,6 @@
 
 def splat(value, shape=(1, 128)):
     return jnp.full(shape, value, jnp.float32)
-
-
-def size_of(lengths, counts, cls):
-    return splat(lengths[cls].astype(jnp.float32)) / splat(counts[cls].astype(jnp.float32))
 
 
 def folded(plane):
@@ -66,48 +62,75 @@
     return core, 1 - core
 
 
-def edges_kernel(lengths, counts, types, q, fields, outward, inward, ends, sems):
+def edges_kernel(
+    lengths,
+    counts,
+    types,
+    q,
+    fields,
+    outward,
+    inward,
+    params,
+    kinds,
+    ends,
+    raw,
+    own_lengths,
+    own_counts,
+    own_types,
+    sems,
+):
     planes = q.shape[0]
     depth = types.shape[0]
     cls = own_class()
-    kind = types[0, cls]
-    rest = depth - 1
     messages = (outward, inward)
-    copies = []
+    copies = [(lengths, own_lengths), (counts, own_counts), (types, own_types)]
     for m, upper in enumerate(sides()):
-        start, turn = upper * (planes - depth) + (1 - upper) * rest, 2 * upper - 1
+        start, turn = upper * (planes - depth) + (1 - upper) * (depth - 1), 2 * upper - 1
         for r in range(depth):
             at = start + turn * r
             copies.append((q.at[at], ends.at[m, r]))
-            if r == 0:
-                copies.append((fields.at[kind, at], messages[m].at[0]))
-            else:
-                for t in range(2):
-                    copies.append((fields.at[t, at], messages[m].at[depth + t * rest + r - 1]))
+            for t in range(2):
+                to = raw.at[m, 2 * r + t] if r < 2 else messages[m].at[depth + 1 + 2 * (r - 2) + t]
+                copies.append((fields.at[t, at], to))
     copies = [pltpu.make_async_copy(a, b, sems.at[i]) for i, (a, b) in enumerate(copies)]
     for copy in copies:
         copy.start()
-    scale = -0.5 * size_of(lengths, counts, cls)
-    for copy in copies:
+    for copy in copies[:3]:
         copy.wait()
-    ours = depth + kind * rest
+    whole = own_lengths[0]
+    for c in range(1, own_lengths.shape[0]):
+        whole = whole + own_lengths[c]
+    length = splat(own_lengths[cls].astype(jnp.float32))
+    size = length / splat(own_counts[cls].astype(jnp.float32))
+    fraction = length / splat(whole.astype(jnp.float32))
+    params[0:1] = size
+    params[1:2] = fraction * size
+    for s in range(depth):
+        kinds[s] = own_types[s, cls]
+    first, second = own_types[0, cls], own_types[1, cls]
+    scale = -0.5 * size
+    for copy in copies[3:]:
+        copy.wait()
     for m, message in enumerate(messages):
         for r in range(depth):
-            chosen = message[0] if r == 0 else message[ours + r - 1]
+            chosen = raw[m, 2 * r + first] if r < 2 else message[depth + 1 + 2 * (r - 2) + first]
             message[r] = jnp.exp(scale * chosen) * ends[m, r].astype(jnp.float32)
+        message[depth] = jnp.exp(scale * (raw[m, 2 + first] + raw[m, 2 + second]))
 
 
 def inner_kernel(
-    lengths, counts, types, q, back, fields, half, state, dens, middle, sums, w, total
+    kinds, params, q, fields, source, half, state, dens, middle, sums, margin, w, total, back, sems
 ):
     planes, nx, ny = q.shape
     depth = back.shape[0]
-    cls = own_class()
-    size = size_of(lengths, counts, cls)
+    copies = [pltpu.make_async_copy(source.at[s], back.at[s], sems.at[s]) for s in range(depth)]
+    for copy in copies:
+        copy.start()
+    size = params[0:1]
     spread = diffusion_scale * size
     keep = 1.0 - 6.0 * spread
     scale = -0.5 * size
-    kinds = [types[s, cls] for s in range(depth)]
+    kinds = [kinds[s] for s in range(depth)]
     edge_low, edge_high = lane_edges(nx, ny)
     clear_margins(w, nx)
     total[...] = jnp.zeros_like(total)
@@ -127,6 +150,7 @@
         now, later = s % 2, (s + 1) % 2
         kind = kinds[s]
         last = s == depth - 1
+        copies[s].wait()
         for i, p in enumerate((s, s + 1, planes - 1 - s, planes - 2 - s)):
             state[s, i] = w[now, p, rows, :]
 
@@ -145,21 +169,23 @@
         lax.fori_loop(s + 1, planes - 1 - s, each, 0, unroll=UNROLL)
         if s == 0:
             sums[0] = total[...]
+        for p in range(depth):
+            margin[s, p] = back[s, p]
+            margin[s, depth + p] = back[s, planes - 1 - p]
     sums[1] = total[...]
 
 
 def outer_kernel(
-    lengths,
-    counts,
-    types,
+    kinds,
+    params,
     outer,
     near,
-    back,
     half,
     state,
     dens,
     middle,
     inner_sums,
+    margin,
     final,
     edge_dens,
     sums,
@@ -167,16 +193,15 @@
     total,
 ):
     planes, nx, ny = final.shape
-    depth = back.shape[0]
-    cls = own_class()
+    depth = margin.shape[0]
     slab = lax.axis_index(SLAB)
     inside = jnp.logical_and(slab > 0, slab < lax.axis_size(SLAB) - 1)
     inside = splat(jnp.where(inside, 1.0, 0.0))
-    size = size_of(lengths, counts, cls)
+    size = params[0:1]
     spread = diffusion_scale * size
     keep = 1.0 - 6.0 * spread
     scale = -0.5 * size
-    kinds = [types[s, cls] for s in range(depth)]
+    kinds = [kinds[s] for s in range(depth)]
     edge_low, edge_high = lane_edges(nx, ny)
     for side in range(2):
         clear_margins(w.at[side], nx)
@@ -192,7 +217,7 @@
     def half_of(m, r, kind):
         if r >= depth:
             return half[kind, place(m, r)]
-        return jnp.exp(scale * came[m][depth + kind * rest + r - 1])
+        return jnp.exp(scale * came[m][depth + 1 + 2 * (r - 2) + kind])
 
     for m in range(2):
         for r in range(depth):
@@ -210,10 +235,14 @@
             for m in range(2):
                 r = s + 1 + i
                 core, beside = neighbours(w, (m, now), r, edge_low, edge_high, nx)
-                fresh = half_of(m, r, kinds[s]) * (keep * core + spread * beside)
+                fresh = keep * core + spread * beside
+                if r == 1:
+                    fresh = came[m][depth] * fresh
+                else:
+                    fresh = half_of(m, r, kinds[s]) * fresh
                 if r >= depth:
                     at = place(m, r)
-                    product = fresh * back[s, at].astype(jnp.float32)
+                    product = fresh * margin[s, upper[m] * depth + r - depth].astype(jnp.float32)
                     edge_dens[upper[m] * depth + r - depth, kinds[s]] += product
                     total[...] += folded(product)
                     if s == rest:
@@ -221,7 +250,9 @@
                 elif m == 0:
                     fresh = inside * fresh
                 if s < rest:
-                    w[m, later, r, rows, :] = half_of(m, r, kinds[s + 1]) * fresh
+                    if r > 1:
+                        fresh = half_of(m, r, kinds[s + 1]) * fresh
+                    w[m, later, r, rows, :] = fresh
         if s == 0:
             part = jnp.sum(inner_sums[0] + total[...], axis=0, keepdims=True)
     whole = jnp.sum(inner_sums[1] + total[...], axis=0, keepdims=True)
@@ -231,18 +262,12 @@
         final[depth + p] = middle[p]
 
 
-def weigh_kernel(cells, lengths, counts, sums, dens, edge_dens, out, extra):
+def weigh_kernel(cells, params, sums, dens, edge_dens, out, extra):
     planes, _, nx, ny = dens.shape
     depth = edge_dens.shape[0] // 2
-    cls = own_class()
-    size = size_of(lengths, counts, cls)
-    whole = lengths[0]
-    for c in range(1, lengths.shape[0]):
-        whole = whole + lengths[c]
-    fraction = splat(lengths[cls].astype(jnp.float32)) / splat(whole.astype(jnp.float32))
     both = jnp.sum(sums[...], axis=0)
     partition = jnp.sum(both[0:1]) / cells
-    weight = fraction * size / splat(partition)
+    weight = params[1:2] / splat(partition)
     first_row = lax.broadcasted_iota(jnp.int32, extra.shape, 0) == 0
     extra[...] = jnp.where(first_row, weight * both[1:2], 0.0)
 
@@ -251,7 +276,7 @@
             out[p, t * nx : (t + 1) * nx, :] = weight * dens[p, t]
         return carry
 
-    lax.fori_loop(depth, planes - depth, body, 0, unroll=2)
+    lax.fori_loop(depth, planes - depth, body, 0, unroll=True)
 
     def ends(p, carry):
         for t in range(2):
@@ -259,7 +284,7 @@
             out[planes - 1 - p, t * nx : (t + 1) * nx, :] = weight * edge_dens[depth + p, t]
         return carry
 
-    lax.fori_loop(0, depth, ends, 0)
+    lax.fori_loop(0, depth, ends, 0, unroll=True)
 
 
 def reduce_kernel(arrived, extra, out):
@@ -291,7 +316,7 @@
     lax.fori_loop(0, planes, body, 0, unroll=2)
 
 
-def call(kernel, outs, scratch, args, smem, flops, name, vmem=2, hbm=0):
+def call(kernel, outs, scratch, args, smem, flops, name, vmem=2, hbm=0, kinds=False):
     size = sum(a.size * a.dtype.itemsize for a in args) + sum(
         o.size * o.dtype.itemsize for o in outs
     )
@@ -300,12 +325,16 @@
         kernel,
         out_shape=outs,
         in_specs=[SMEM] * smem + [VMEM] * (len(args) - smem - hbm) + [anywhere] * hbm,
-        out_specs=[VMEM] * len(outs),
+        out_specs=[VMEM] * (len(outs) - kinds) + [SMEM] * kinds,
         scratch_shapes=scratch,
-        compiler_params=pltpu.CompilerParams(vmem_limit_bytes=vmem and vmem * 2**20),
+        compiler_params=pltpu.CompilerParams(vmem_limit_bytes=vmem * 2**20),
         cost_estimate=pl.CostEstimate(flops=flops, bytes_accessed=size, transcendentals=0),
         name=name,
     )(*args)
+
+
+def in_hbm(x):
+    return pltpu.with_memory_space_constraint(x, pltpu.HBM)
 
 
 def f32(*shape):
@@ -320,18 +349,27 @@
     types = types.T
     peers = lax.axis_size(XY)
     slabs = lax.axis_size(SLAB)
-    message = f32(3 * depth - 2, nx, ny)
-
-    outward, inward = call(
+    message = f32(3 * depth - 3, nx, ny)
+    classes = lengths.shape[0]
+
+    outward, inward, params, kinds = call(
         edges_kernel,
-        [message, message],
-        [pltpu.VMEM((2, depth, nx, ny), jnp.bfloat16), pltpu.SemaphoreType.DMA((2 * (3 * depth - 1),))],
-        (lengths, counts, types, q, fields),
-        3,
+        [message, message, f32(8, ny), jax.ShapeDtypeStruct((depth,), jnp.int32)],
+        [
+            pltpu.VMEM((2, depth, nx, ny), jnp.bfloat16),
+            pltpu.VMEM((2, 4, nx, ny), jnp.float32),
+            pltpu.SMEM((classes,), jnp.int32),
+            pltpu.SMEM((classes,), jnp.int32),
+            pltpu.SMEM((depth, classes), jnp.int32),
+            pltpu.SemaphoreType.DMA((6 * depth + 3,)),
+        ],
+        tuple(map(in_hbm, (lengths, counts, types, q, fields))),
+        0,
         10**6,
         "edges",
-        vmem=None,
-        hbm=2,
+        vmem=4,
+        hbm=5,
+        kinds=True,
     )
     across = [(i, i + 1) for i in range(1, slabs - 1, 2)]
     within = [(i, i + 1) for i in range(0, slabs, 2)]
@@ -339,7 +377,7 @@
     near = lax.ppermute(inward, SLAB, within + [(b, a) for a, b in within])
 
     padded = nx + 2 * TOP
-    half, state, dens, middle, sums = call(
+    half, state, dens, middle, sums, margin = call(
         inner_kernel,
         [
             f32(2, planes, nx, ny),
@@ -347,16 +385,20 @@
             f32(planes, 2, nx, ny),
             jax.ShapeDtypeStruct((planes - 2 * depth, nx, ny), jnp.bfloat16),
             f32(2, 8, ny),
+            jax.ShapeDtypeStruct((depth, 2 * depth, nx, ny), back.dtype),
         ],
         [
             pltpu.VMEM((2, planes, padded, ny), jnp.float32),
             pltpu.VMEM((8, ny), jnp.float32),
+            pltpu.VMEM(back.shape, back.dtype),
+            pltpu.SemaphoreType.DMA((depth,)),
         ],
-        (lengths, counts, types, q, back, fields),
-        3,
+        (kinds, params, q, fields, in_hbm(back)),
+        1,
         10**8,
         "inner",
         vmem=8,
+        hbm=1,
     )
     final, edge_dens, sums = call(
         outer_kernel,
@@ -369,8 +411,8 @@
             pltpu.VMEM((2, 2, 2 * depth + 2, padded, ny), jnp.float32),
             pltpu.VMEM((8, ny), jnp.float32),
         ],
-        (lengths, counts, types, outer, near, back, half, state, dens, middle, sums),
-        3,
+        (kinds, params, outer, near, half, state, dens, middle, sums, margin),
+        1,
         10**8,
         "outer",
         vmem=8,
@@ -380,8 +422,8 @@
         functools.partial(weigh_kernel, cells),
         [f32(peers, 2 * nx, ny), f32(8, ny)],
         [],
-        (lengths, counts, sums, dens, edge_dens),
-        2,
+        (params, sums, dens, edge_dens),
+        0,
         10**6,
         "weigh",
         vmem=8,

time: 101 us -> 98.5 us (0.975)
  local copies, waits for them, and re-layouts: 1.24 us -> 0.01 us
  Pallas kernels: 9.28 us -> 8.26 us
    unnamed x14 -> x4, local copies, waits for them, and re-layouts: 1.24 us -> 0.01 us
    pallas_call x7, Pallas kernels: 9.28 us -> 8.26 us  [call(): pl.pallas_call(kernel, out_shape=outs, in_specs=[SMEM] * smem + [VMEM] *...]
  transfers between devices with their start and end apart: 2 -> 2, of which waited for: 0 -> 0; matrix products, arithmetic and copies ran while one was open for 0% -> 0% of each run, Pallas kernels for 2% -> 3%
where the time goes in v5:
time: 98.5 us; the launch traced here: 98.2 us
  blocking collectives  83.4 us (85%)
  Pallas kernels  8.26 us (8%)
  starting transfers between devices  5.85 us (6%)
    all_to_all x1, blocking collectives, body(): arrived = lax.all_to_all(sent, XY, 0, 0, tiled=True)  24.3 us
    all_to_all x1, blocking collectives, body(): blocks = lax.all_to_all(blocks, XY, 0, 0, tiled=True)  21.6 us
    all_to_all x1, blocking collectives, body(): sums = lax.all_to_all(sums, SLAB, 0, 0, tiled=True)  20.9 us
    all_gather x1, blocking collectives, body(): pair = lax.all_gather(own, 'zh', axis=0, tiled=False)  16.7 us
    pallas_call x7, Pallas kernels, call(): pl.pallas_call(kernel, out_shape=outs, in_specs=[SMEM] * smem + [VMEM] *...  8.26 us
    ppermute x1, starting transfers between devices, body(): near = lax.ppermute(inward, SLAB, within + [(b, a) for a, b in within])  3.93 us
  transfers between devices with their start and end apart: 2, of which 0 were waited for; matrix products, arithmetic and copies ran while one was open for 0% of the time, Pallas kernels for 3%

profile of v5, /device:TPU:32, one launch (start us, length us, event | category | flops | bytes accessed | tf_op | source)
XLA Modules:
  0.0 98.2 jit_solution(10541075566304080598)
XLA Ops:
  0.6 0.0 copy-start
  0.6 0.0 copy-start.1
  0.7 2.0 %edges.1 = (f32[9,64,128]{2,1,0:T(8,128)S(1)}, f32[9,64,128]{2,1,0:T(8,128)S(1)}, f32[8,128]{1,0:T(8,128)S(1)}, s32[4]{0:T(128)S(1)}) custom-call(s32[32]{0:T(128)} %lengths.1, s32[32]{0:T(128)} %counts.1, s32[4,32]{1,0:T(4,128)} %bitcast.9, bf16[16,64,128]{2,1,0:T(8,128)(2,1)} %bitcast.5, f32[2,16,64,128]{3,2,1,0:T(8,128)} %fields.5), custom_call_target="tpu_custom_call" | custom-call | flops 1000000 | bytes 1905424 | tf_op jit(solution)/shard_map/edges/pallas_call | solution.py:324
  2.7 1.9 %collective-permute-start = (f32[9,64,128]{2,1,0:T(8,128)S(1)}, f32[9,64,128]{2,1,0:T(8,128)S(1)}, u32[]{:S(2)}, u32[]{:S(2)}) collective-permute-start(f32[9,64,128]{2,1,0:T(8,128)S(1)} %get-tuple-element.19), channel_id=1, source_target_pairs={{1,2},{3,4},{5,6},{7,8},{9,10},{11,12},{13,14},{2,1},{4,3},{6,5},{... | collective-permute-start | bytes 884744 | tf_op jit(solution)/shard_map/ppermute | solution.py:376
  4.6 3.9 %collective-permute-start.1 = (f32[9,64,128]{2,1,0:T(8,128)S(1)}, f32[9,64,128]{2,1,0:T(8,128)S(1)}, u32[]{:S(2)}, u32[]{:S(2)}) collective-permute-start(f32[9,64,128]{2,1,0:T(8,128)S(1)} %get-tuple-element.20), channel_id=1, source_target_pairs={{0,1},{2,3},{4,5},{6,7},{8,9},{10,11},{12,13},{14,15},{1,0},{3,2},... | collective-permute-start | bytes 884744 | tf_op jit(solution)/shard_map/ppermute | solution.py:377
  8.5 0.0 copy-done
  8.5 0.0 copy-done.1
  8.5 2.6 %inner.1 = (f32[2,16,64,128]{3,2,1,0:T(8,128)S(1)}, f32[4,4,64,128]{3,2,1,0:T(8,128)S(1)}, f32[16,2,64,128]{3,2,1,0:T(8,128)S(1)}, bf16[8,64,128]{2,1,0:T(8,128)...) custom-call(s32[4]{0:T(128)S(1)} %get-tuple-element.18.kinds, ...), custom_call_target="tpu_custom_call" | custom-call | flops 100000000 | bytes 5648400 | tf_op jit(solution)/shard_map/inner/pallas_call | solution.py:324
  11.2 0.0 collective-permute-done.outer
  11.2 0.0 collective-permute-done.1.near
  11.2 2.0 %outer.1 = (bf16[16,64,128]{2,1,0:T(8,128)(2,1)}, f32[8,2,64,128]{3,2,1,0:T(8,128)S(1)}, f32[16,2,128]{2,1,0:T(2,128)S(1)}) custom-call(s32[4]{0:T(128)S(1)} %get-tuple-element.18.kinds, f32[8,128]{1,0:T(8,128)S(1)} %get-tuple-element.17.params, f32[9,64,128]{2,1,0:T(8,128)S(1)} %collective-permute-done.outer, ...), custom_call_target="tpu_custom_call" | custom-call | flops 100000000 | bytes 4681744 | tf_op jit(solution)/shard_map/outer/pallas_call | solution.py:324
  13.1 20.9 %all_to_all.15.sums = f32[16,2,128]{2,1,0:T(2,128)S(1)} all-to-all(f32[16,2,128]{2,1,0:T(2,128)S(1)} %get-tuple-element.27), channel_id=1, replica_groups=mesh['zh'=2,'y'=4,'x'=4,'slab'=16] {'slab'}, dimensions={0} | all-to-all | bytes 32768 | tf_op jit(solution)/shard_map/all_to_all | solution.py:420
  34.0 0.2 weigh.1
  34.2 24.3 %all_to_all.16.arrived = f32[16,128,128]{2,1,0:T(8,128)S(1)} all-to-all(f32[16,128,128]{2,1,0:T(8,128)S(1)} %get-tuple-element.29), channel_id=1, replica_groups=mesh['zh'=2,'y'=4,'x'=4,'slab'=16] {'y','x'}, dimensions={0} | all-to-all | bytes 2097152 | tf_op jit(solution)/shard_map/all_to_all | solution.py:431
  58.5 0.1 reduce.1
  58.6 16.7 %all-gather = f32[272,128]{1,0:T(8,128)S(1)} all-gather(f32[136,128]{1,0:T(8,128)S(1)} %reduce.1), channel_id=2, replica_groups=mesh['zh'=2,'y'=4,'x'=4,'slab'=16] {'zh'}, dimensions={0}, use_global_device_ids=true | all-gather | bytes 208896 | tf_op jit(solution)/shard_map/all_gather | solution.py:435
  75.2 0.1 spread.1
  75.3 21.6 %all_to_all.17.blocks = f32[16,136,128]{2,1,0:T(8,128)S(1)} all-to-all(f32[16,136,128]{2,1,0:T(8,128)S(1)} %spread.1), channel_id=1, replica_groups=mesh['zh'=2,'y'=4,'x'=4,'slab'=16] {'y','x'}, dimensions={0} | all-to-all | bytes 2228224 | tf_op jit(solution)/shard_map/all_to_all | solution.py:439
  96.9 1.4 %update.1 = f32[2,16,64,128]{3,2,1,0:T(8,128)} custom-call(f32[16,136,128]{2,1,0:T(8,128)S(1)} %all_to_all.17.blocks, f32[2,16,64,128]{3,2,1,0:T(8,128)S(1)} %copy-done), custom_call_target="tpu_custom_call" | custom-call | flops 1000000 | bytes 3211264 | tf_op jit(solution)/shard_map/update/pallas_call | solution.py:324
Async XLA Ops:
  0.6 7.9 %copy-start = (f32[2,16,64,128]{3,2,1,0:T(8,128)S(1)}, f32[2,16,64,128]{3,2,1,0:T(8,128)}, u32[]{:S(2)}) copy-start(f32[2,16,64,128]{3,2,1,0:T(8,128)} %fields.5) | copy-start | bytes 3145732
  0.6 7.9 %copy-start.1 = (bf16[1,16,64,128]{3,2,1,0:T(8,128)(2,1)S(1)}, bf16[1,16,64,128]{3,2,1,0:T(8,128)(2,1)}, u32[]{:S(2)}) copy-start(bf16[1,16,64,128]{3,2,1,0:T(8,128)(2,1)} %param.6) | copy-start | bytes 786436
  2.7 8.5 %collective-permute-start = (f32[9,64,128]{2,1,0:T(8,128)S(1)}, f32[9,64,128]{2,1,0:T(8,128)S(1)}, u32[]{:S(2)}, u32[]{:S(2)}) collective-permute-start(f32[9,64,128]{2,1,0:T(8,128)S(1)} %get-tuple-element.19), channel_id=1, source_target_pairs={{1,2},{3,4},{5,6},{7,8},{9,10},{11,12},{13,14},{2,1},{4,3},{6,5},{... | collective-permute-start | bytes 884744 | tf_op jit(solution)/shard_map/ppermute | solution.py:376
  4.6 6.6 %collective-permute-start.1 = (f32[9,64,128]{2,1,0:T(8,128)S(1)}, f32[9,64,128]{2,1,0:T(8,128)S(1)}, u32[]{:S(2)}, u32[]{:S(2)}) collective-permute-start(f32[9,64,128]{2,1,0:T(8,128)S(1)} %get-tuple-element.20), channel_id=1, source_target_pairs={{0,1},{2,3},{4,5},{6,7},{8,9},{10,11},{12,13},{14,15},{1,0},{3,2},... | collective-permute-start | bytes 884744 | tf_op jit(solution)/shard_map/ppermute | solution.py:377

commit v6 on v5

--- a/solution.py
+++ b/solution.py
@@ -191,8 +191,17 @@
     sums,
     w,
     total,
+    last,
+    sems,
 ):
     planes, nx, ny = final.shape
+    kept = middle.shape[0]
+    copies = [
+        pltpu.make_async_copy(
+            middle, final.at[pl.ds((planes - kept) // 2, kept)], sems.at[2]
+        )
+    ]
+    copies[0].start()
     depth = margin.shape[0]
     slab = lax.axis_index(SLAB)
     inside = jnp.logical_and(slab > 0, slab < lax.axis_size(SLAB) - 1)
@@ -246,7 +255,9 @@
                     edge_dens[upper[m] * depth + r - depth, kinds[s]] += product
                     total[...] += folded(product)
                     if s == rest:
-                        final[at] = fresh.astype(jnp.bfloat16)
+                        last[upper[m] * depth + at - upper[m] * (planes - depth)] = fresh.astype(
+                            jnp.bfloat16
+                        )
                 elif m == 0:
                     fresh = inside * fresh
                 if s < rest:
@@ -255,44 +266,43 @@
                     w[m, later, r, rows, :] = fresh
         if s == 0:
             part = jnp.sum(inner_sums[0] + total[...], axis=0, keepdims=True)
+    for side in range(2):
+        to = final.at[pl.ds(side * (planes - depth), depth)]
+        copy = pltpu.make_async_copy(last.at[pl.ds(side * depth, depth)], to, sems.at[side])
+        copy.start()
+        copies.append(copy)
     whole = jnp.sum(inner_sums[1] + total[...], axis=0, keepdims=True)
     both = jnp.concatenate([part, whole], 0)
     sums[...] = jnp.broadcast_to(both[None], sums.shape)
-    for p in range(planes - 2 * depth):
-        final[depth + p] = middle[p]
-
-
-def weigh_kernel(cells, params, sums, dens, edge_dens, out, extra):
+    for copy in copies:
+        copy.wait()
+
+
+def weigh_kernel(cells, params, sums, dens, edge_dens, out):
     planes, _, nx, ny = dens.shape
     depth = edge_dens.shape[0] // 2
     both = jnp.sum(sums[...], axis=0)
     partition = jnp.sum(both[0:1]) / cells
     weight = params[1:2] / splat(partition)
-    first_row = lax.broadcasted_iota(jnp.int32, extra.shape, 0) == 0
-    extra[...] = jnp.where(first_row, weight * both[1:2], 0.0)
-
-    def body(p, carry):
+    level = weight * (jnp.sum(both[1:2]) / cells)
+    shift = level * (stiffness / (flory_chi + 2.0 * stiffness))
+
+    for p in range(planes):
         for t in range(2):
-            out[p, t * nx : (t + 1) * nx, :] = weight * dens[p, t]
-        return carry
-
-    lax.fori_loop(depth, planes - depth, body, 0, unroll=True)
-
-    def ends(p, carry):
-        for t in range(2):
-            out[p, t * nx : (t + 1) * nx, :] = weight * edge_dens[p, t]
-            out[planes - 1 - p, t * nx : (t + 1) * nx, :] = weight * edge_dens[depth + p, t]
-        return carry
-
-    lax.fori_loop(0, depth, ends, 0, unroll=True)
-
-
-def reduce_kernel(arrived, extra, out):
+            if p < depth:
+                mine = edge_dens[p, t]
+            elif p >= planes - depth:
+                mine = edge_dens[depth + planes - 1 - p, t]
+            else:
+                mine = dens[p, t]
+            out[p, t * nx : (t + 1) * nx, :] = weight * mine - shift
+
+
+def reduce_kernel(arrived, out):
     acc = arrived[0]
     for c in range(1, arrived.shape[0]):
         acc = acc + arrived[c]
-    out[0 : acc.shape[0]] = acc
-    out[acc.shape[0] :] = extra[...]
+    out[...] = acc
 
 
 def spread_kernel(pair, blocks):
@@ -300,23 +310,28 @@
     blocks[...] = jnp.broadcast_to(both[None], blocks.shape)
 
 
-def update_kernel(cells, blocks, fields, out):
+def update_kernel(blocks, fields, out, fresh, sems):
     _, planes, nx, ny = fields.shape
-    level = splat(jnp.sum(jnp.sum(blocks[:, 2 * nx :], axis=0)) / cells)
-
-    def body(p, carry):
-        first, second = blocks[p, 0:nx, :], blocks[p, nx : 2 * nx, :]
-        pressure = stiffness * (first + second - level)
-        old = fields[0, p]
-        out[0, p] = old + mixing * (flory_chi * second + pressure - old)
-        old = fields[1, p]
-        out[1, p] = old + mixing * (flory_chi * first + pressure - old)
-        return carry
-
-    lax.fori_loop(0, planes, body, 0, unroll=2)
-
-
-def call(kernel, outs, scratch, args, smem, flops, name, vmem=2, hbm=0, kinds=False):
+    chunk = planes // sems.shape[0]
+    copies = []
+    for i in range(sems.shape[0]):
+        for p in range(i * chunk, (i + 1) * chunk):
+            first, second = blocks[p, 0:nx, :], blocks[p, nx : 2 * nx, :]
+            pressure = stiffness * (first + second)
+            old = fields[0, p]
+            fresh[0, p] = old + mixing * (flory_chi * second + pressure - old)
+            old = fields[1, p]
+            fresh[1, p] = old + mixing * (flory_chi * first + pressure - old)
+        at = pl.ds(i * chunk, chunk)
+        for t in range(2):
+            copy = pltpu.make_async_copy(fresh.at[t, at], out.at[t, at], sems.at[i, t])
+            copy.start()
+            copies.append(copy)
+    for copy in copies:
+        copy.wait()
+
+
+def call(kernel, outs, scratch, args, smem, flops, name, vmem=2, hbm=0, kinds=False, far=()):
     size = sum(a.size * a.dtype.itemsize for a in args) + sum(
         o.size * o.dtype.itemsize for o in outs
     )
@@ -325,7 +340,8 @@
         kernel,
         out_shape=outs,
         in_specs=[SMEM] * smem + [VMEM] * (len(args) - smem - hbm) + [anywhere] * hbm,
-        out_specs=[VMEM] * (len(outs) - kinds) + [SMEM] * kinds,
+        out_specs=[anywhere if i in far else VMEM for i in range(len(outs) - kinds)]
+        + [SMEM] * kinds,
         scratch_shapes=scratch,
         compiler_params=pltpu.CompilerParams(vmem_limit_bytes=vmem * 2**20),
         cost_estimate=pl.CostEstimate(flops=flops, bytes_accessed=size, transcendentals=0),
@@ -410,17 +426,20 @@
         [
             pltpu.VMEM((2, 2, 2 * depth + 2, padded, ny), jnp.float32),
             pltpu.VMEM((8, ny), jnp.float32),
+            pltpu.VMEM((2 * depth, nx, ny), jnp.bfloat16),
+            pltpu.SemaphoreType.DMA((3,)),
         ],
         (kinds, params, outer, near, half, state, dens, middle, sums, margin),
         1,
         10**8,
         "outer",
         vmem=8,
+        far=(0,),
     )
     sums = lax.all_to_all(sums, SLAB, 0, 0, tiled=True)
-    sent, extra = call(
+    (sent,) = call(
         functools.partial(weigh_kernel, cells),
-        [f32(peers, 2 * nx, ny), f32(8, ny)],
+        [f32(peers, 2 * nx, ny)],
         [],
         (params, sums, dens, edge_dens),
         0,
@@ -429,23 +448,25 @@
         vmem=8,
     )
     arrived = lax.all_to_all(sent, XY, 0, 0, tiled=True)
-    (own,) = call(
-        reduce_kernel, [f32(2 * nx + 8, ny)], [], (arrived, extra), 0, 10**6, "reduce", vmem=8
-    )
+    (own,) = call(reduce_kernel, [f32(2 * nx, ny)], [], (arrived,), 0, 10**6, "reduce", vmem=8)
     pair = lax.all_gather(own, "zh", axis=0, tiled=False)
     (blocks,) = call(
-        spread_kernel, [f32(peers, 2 * nx + 8, ny)], [], (pair,), 0, 10**6, "spread", vmem=8
+        spread_kernel, [f32(peers, 2 * nx, ny)], [], (pair,), 0, 10**6, "spread", vmem=8
     )
     blocks = lax.all_to_all(blocks, XY, 0, 0, tiled=True)
     (fields_new,) = call(
-        functools.partial(update_kernel, cells),
+        update_kernel,
         [f32(2, planes, nx, ny)],
-        [],
+        [
+            pltpu.VMEM((2, planes, nx, ny), jnp.float32),
+            pltpu.SemaphoreType.DMA((4, 2)),
+        ],
         (blocks, fields),
         0,
         10**6,
         "update",
         vmem=8,
+        far=(0,),
     )
     return fields_new, final[None]
 

time: 98.5 us -> 97.2 us (0.987)
  blocking collectives: 83.4 us -> 82.3 us
where the time goes in v6:
time: 97.2 us; the launch traced here: 96.9 us
  blocking collectives  82.3 us (85%)
  Pallas kernels  8 us (8%)
  starting transfers between devices  5.85 us (6%)
    all_to_all x1, blocking collectives, body(): arrived = lax.all_to_all(sent, XY, 0, 0, tiled=True)  24.3 us
    all_to_all x1, blocking collectives, body(): sums = lax.all_to_all(sums, SLAB, 0, 0, tiled=True)  20.9 us
    all_to_all x1, blocking collectives, body(): blocks = lax.all_to_all(blocks, XY, 0, 0, tiled=True)  20.9 us
    all_gather x1, blocking collectives, body(): pair = lax.all_gather(own, 'zh', axis=0, tiled=False)  16.3 us
    pallas_call x7, Pallas kernels, call(): pl.pallas_call(kernel, out_shape=outs, in_specs=[SMEM] * smem + [VMEM] *...  8 us
    ppermute x1, starting transfers between devices, body(): near = lax.ppermute(inward, SLAB, within + [(b, a) for a, b in within])  3.93 us
  transfers between devices with their start and end apart: 2, of which 0 were waited for; matrix products, arithmetic and copies ran while one was open for 0% of the time, Pallas kernels for 3%

profile of v6, /device:TPU:32, one launch (start us, length us, event | category | flops | bytes accessed | tf_op | source)
XLA Modules:
  0.0 96.9 jit_solution(9973425671991031951)
XLA Ops:
  0.6 0.0 copy-start
  0.6 0.0 copy-start.1
  0.7 2.0 %edges.1 = (f32[9,64,128]{2,1,0:T(8,128)S(1)}, f32[9,64,128]{2,1,0:T(8,128)S(1)}, f32[8,128]{1,0:T(8,128)S(1)}, s32[4]{0:T(128)S(1)}) custom-call(s32[32]{0:T(128)} %lengths.1, s32[32]{0:T(128)} %counts.1, s32[4,32]{1,0:T(4,128)} %bitcast.9, bf16[16,64,128]{2,1,0:T(8,128)(2,1)} %bitcast.5, f32[2,16,64,128]{3,2,1,0:T(8,128)} %fields.5), custom_call_target="tpu_custom_call" | custom-call | flops 1000000 | bytes 1905424 | tf_op jit(solution)/shard_map/edges/pallas_call | solution.py:339
  2.7 1.9 %collective-permute-start = (f32[9,64,128]{2,1,0:T(8,128)S(1)}, f32[9,64,128]{2,1,0:T(8,128)S(1)}, u32[]{:S(2)}, u32[]{:S(2)}) collective-permute-start(f32[9,64,128]{2,1,0:T(8,128)S(1)} %get-tuple-element.17), channel_id=1, source_target_pairs={{1,2},{3,4},{5,6},{7,8},{9,10},{11,12},{13,14},{2,1},{4,3},{6,5},{... | collective-permute-start | bytes 884744 | tf_op jit(solution)/shard_map/ppermute | solution.py:392
  4.6 3.9 %collective-permute-start.1 = (f32[9,64,128]{2,1,0:T(8,128)S(1)}, f32[9,64,128]{2,1,0:T(8,128)S(1)}, u32[]{:S(2)}, u32[]{:S(2)}) collective-permute-start(f32[9,64,128]{2,1,0:T(8,128)S(1)} %get-tuple-element.18), channel_id=1, source_target_pairs={{0,1},{2,3},{4,5},{6,7},{8,9},{10,11},{12,13},{14,15},{1,0},{3,2},... | collective-permute-start | bytes 884744 | tf_op jit(solution)/shard_map/ppermute | solution.py:393
  8.5 0.0 copy-done
  8.5 0.0 copy-done.1
  8.5 2.6 %inner.1 = (f32[2,16,64,128]{3,2,1,0:T(8,128)S(1)}, f32[4,4,64,128]{3,2,1,0:T(8,128)S(1)}, f32[16,2,64,128]{3,2,1,0:T(8,128)S(1)}, bf16[8,64,128]{2,1,0:T(8,128)...) custom-call(s32[4]{0:T(128)S(1)} %get-tuple-element.16.kinds, ...), custom_call_target="tpu_custom_call" | custom-call | flops 100000000 | bytes 5648400 | tf_op jit(solution)/shard_map/inner/pallas_call | solution.py:339
  11.2 0.0 collective-permute-done.outer
  11.2 0.0 collective-permute-done.1.near
  11.2 2.0 %outer.1 = (bf16[16,64,128]{2,1,0:T(8,128)(2,1)}, f32[8,2,64,128]{3,2,1,0:T(8,128)S(1)}, f32[16,2,128]{2,1,0:T(2,128)S(1)}) custom-call(s32[4]{0:T(128)S(1)} %get-tuple-element.16.kinds, f32[8,128]{1,0:T(8,128)S(1)} %get-tuple-element.15.params, f32[9,64,128]{2,1,0:T(8,128)S(1)} %collective-permute-done.outer, ...), custom_call_target="tpu_custom_call" | custom-call | flops 100000000 | bytes 4681744 | tf_op jit(solution)/shard_map/outer/pallas_call | solution.py:339
  13.1 20.9 %all_to_all.15.sums = f32[16,2,128]{2,1,0:T(2,128)S(1)} all-to-all(f32[16,2,128]{2,1,0:T(2,128)S(1)} %get-tuple-element.25), channel_id=1, replica_groups=mesh['zh'=2,'y'=4,'x'=4,'slab'=16] {'slab'}, dimensions={0} | all-to-all | bytes 32768 | tf_op jit(solution)/shard_map/all_to_all | solution.py:439
  34.0 0.2 weigh.1
  34.3 24.3 %all_to_all.16.arrived = f32[16,128,128]{2,1,0:T(8,128)S(1)} all-to-all(f32[16,128,128]{2,1,0:T(8,128)S(1)} %weigh.1), channel_id=1, replica_groups=mesh['zh'=2,'y'=4,'x'=4,'slab'=16] {'y','x'}, dimensions={0} | all-to-all | bytes 2097152 | tf_op jit(solution)/shard_map/all_to_all | solution.py:450
  58.5 0.1 reduce.1
  58.6 16.3 %all-gather = f32[256,128]{1,0:T(8,128)S(1)} all-gather(f32[128,128]{1,0:T(8,128)S(1)} %reduce.1), channel_id=2, replica_groups=mesh['zh'=2,'y'=4,'x'=4,'slab'=16] {'zh'}, dimensions={0}, use_global_device_ids=true | all-gather | bytes 196608 | tf_op jit(solution)/shard_map/all_gather | solution.py:452
  74.9 0.1 spread.1
  75.0 20.9 %all_to_all.17.blocks = f32[16,128,128]{2,1,0:T(8,128)S(1)} all-to-all(f32[16,128,128]{2,1,0:T(8,128)S(1)} %spread.1), channel_id=1, replica_groups=mesh['zh'=2,'y'=4,'x'=4,'slab'=16] {'y','x'}, dimensions={0} | all-to-all | bytes 2097152 | tf_op jit(solution)/shard_map/all_to_all | solution.py:456
  95.9 1.1 %update.1 = f32[2,16,64,128]{3,2,1,0:T(8,128)} custom-call(f32[16,128,128]{2,1,0:T(8,128)S(1)} %all_to_all.17.blocks, f32[2,16,64,128]{3,2,1,0:T(8,128)S(1)} %copy-done), custom_call_target="tpu_custom_call" | custom-call | flops 1000000 | bytes 3145728 | tf_op jit(solution)/shard_map/update/pallas_call | solution.py:339
Async XLA Ops:
  0.6 7.9 %copy-start = (f32[2,16,64,128]{3,2,1,0:T(8,128)S(1)}, f32[2,16,64,128]{3,2,1,0:T(8,128)}, u32[]{:S(2)}) copy-start(f32[2,16,64,128]{3,2,1,0:T(8,128)} %fields.5) | copy-start | bytes 3145732
  0.6 7.9 %copy-start.1 = (bf16[1,16,64,128]{3,2,1,0:T(8,128)(2,1)S(1)}, bf16[1,16,64,128]{3,2,1,0:T(8,128)(2,1)}, u32[]{:S(2)}) copy-start(bf16[1,16,64,128]{3,2,1,0:T(8,128)(2,1)} %param.6) | copy-start | bytes 786436
  2.7 8.5 %collective-permute-start = (f32[9,64,128]{2,1,0:T(8,128)S(1)}, f32[9,64,128]{2,1,0:T(8,128)S(1)}, u32[]{:S(2)}, u32[]{:S(2)}) collective-permute-start(f32[9,64,128]{2,1,0:T(8,128)S(1)} %get-tuple-element.17), channel_id=1, source_target_pairs={{1,2},{3,4},{5,6},{7,8},{9,10},{11,12},{13,14},{2,1},{4,3},{6,5},{... | collective-permute-start | bytes 884744 | tf_op jit(solution)/shard_map/ppermute | solution.py:392
  4.6 6.6 %collective-permute-start.1 = (f32[9,64,128]{2,1,0:T(8,128)S(1)}, f32[9,64,128]{2,1,0:T(8,128)S(1)}, u32[]{:S(2)}, u32[]{:S(2)}) collective-permute-start(f32[9,64,128]{2,1,0:T(8,128)S(1)} %get-tuple-element.18), channel_id=1, source_target_pairs={{0,1},{2,3},{4,5},{6,7},{8,9},{10,11},{12,13},{14,15},{1,0},{3,2},... | collective-permute-start | bytes 884744 | tf_op jit(solution)/shard_map/ppermute | solution.py:393

commit v7 on v6

--- a/solution.py
+++ b/solution.py
@@ -183,25 +183,15 @@
     half,
     state,
     dens,
-    middle,
     inner_sums,
     margin,
-    final,
+    last,
     edge_dens,
     sums,
     w,
     total,
-    last,
-    sems,
 ):
-    planes, nx, ny = final.shape
-    kept = middle.shape[0]
-    copies = [
-        pltpu.make_async_copy(
-            middle, final.at[pl.ds((planes - kept) // 2, kept)], sems.at[2]
-        )
-    ]
-    copies[0].start()
+    _, planes, nx, ny = half.shape
     depth = margin.shape[0]
     slab = lax.axis_index(SLAB)
     inside = jnp.logical_and(slab > 0, slab < lax.axis_size(SLAB) - 1)
@@ -266,16 +256,9 @@
                     w[m, later, r, rows, :] = fresh
         if s == 0:
             part = jnp.sum(inner_sums[0] + total[...], axis=0, keepdims=True)
-    for side in range(2):
-        to = final.at[pl.ds(side * (planes - depth), depth)]
-        copy = pltpu.make_async_copy(last.at[pl.ds(side * depth, depth)], to, sems.at[side])
-        copy.start()
-        copies.append(copy)
     whole = jnp.sum(inner_sums[1] + total[...], axis=0, keepdims=True)
     both = jnp.concatenate([part, whole], 0)
     sums[...] = jnp.broadcast_to(both[None], sums.shape)
-    for copy in copies:
-        copy.wait()
 
 
 def weigh_kernel(cells, params, sums, dens, edge_dens, out):
@@ -310,10 +293,19 @@
     blocks[...] = jnp.broadcast_to(both[None], blocks.shape)
 
 
-def update_kernel(blocks, fields, out, fresh, sems):
+def update_kernel(blocks, fields, middle, last, out, final, fresh, sems, end_sems):
     _, planes, nx, ny = fields.shape
     chunk = planes // sems.shape[0]
+    depth = last.shape[0] // 2
+    parts = (
+        (middle, depth, middle.shape[0]),
+        (last.at[pl.ds(0, depth)], 0, depth),
+        (last.at[pl.ds(depth, depth)], planes - depth, depth),
+    )
     copies = []
+    for i, (part, at, count) in enumerate(parts):
+        copies.append(pltpu.make_async_copy(part, final.at[pl.ds(at, count)], end_sems.at[i]))
+        copies[-1].start()
     for i in range(sems.shape[0]):
         for p in range(i * chunk, (i + 1) * chunk):
             first, second = blocks[p, 0:nx, :], blocks[p, nx : 2 * nx, :]
@@ -416,25 +408,22 @@
         vmem=8,
         hbm=1,
     )
-    final, edge_dens, sums = call(
+    last, edge_dens, sums = call(
         outer_kernel,
         [
-            jax.ShapeDtypeStruct((planes, nx, ny), jnp.bfloat16),
+            jax.ShapeDtypeStruct((2 * depth, nx, ny), jnp.bfloat16),
             f32(2 * depth, 2, nx, ny),
             f32(slabs, 2, ny),
         ],
         [
             pltpu.VMEM((2, 2, 2 * depth + 2, padded, ny), jnp.float32),
             pltpu.VMEM((8, ny), jnp.float32),
-            pltpu.VMEM((2 * depth, nx, ny), jnp.bfloat16),
-            pltpu.SemaphoreType.DMA((3,)),
-        ],
-        (kinds, params, outer, near, half, state, dens, middle, sums, margin),
+        ],
+        (kinds, params, outer, near, half, state, dens, sums, margin),
         1,
         10**8,
         "outer",
         vmem=8,
-        far=(0,),
     )
     sums = lax.all_to_all(sums, SLAB, 0, 0, tiled=True)
     (sent,) = call(
@@ -454,19 +443,20 @@
         spread_kernel, [f32(peers, 2 * nx, ny)], [], (pair,), 0, 10**6, "spread", vmem=8
     )
     blocks = lax.all_to_all(blocks, XY, 0, 0, tiled=True)
-    (fields_new,) = call(
+    fields_new, final = call(
         update_kernel,
-        [f32(2, planes, nx, ny)],
+        [f32(2, planes, nx, ny), jax.ShapeDtypeStruct((planes, nx, ny), jnp.bfloat16)],
         [
             pltpu.VMEM((2, planes, nx, ny), jnp.float32),
             pltpu.SemaphoreType.DMA((4, 2)),
-        ],
-        (blocks, fields),
+            pltpu.SemaphoreType.DMA((3,)),
+        ],
+        (blocks, fields, middle, last),
         0,
         10**6,
         "update",
         vmem=8,
-        far=(0,),
+        far=(0, 1),
     )
     return fields_new, final[None]
 

time: 97.2 us -> 96.7 us (level)
  no operation moved by 1% of the time
where the time goes in v7:
time: 96.7 us; the launch traced here: 96.4 us
  blocking collectives  82.3 us (85%)
  Pallas kernels  7.45 us (8%)
  starting transfers between devices  5.85 us (6%)
    all_to_all x1, blocking collectives, body(): arrived = lax.all_to_all(sent, XY, 0, 0, tiled=True)  24.3 us
    all_to_all x1, blocking collectives, body(): sums = lax.all_to_all(sums, SLAB, 0, 0, tiled=True)  20.9 us
    all_to_all x1, blocking collectives, body(): blocks = lax.all_to_all(blocks, XY, 0, 0, tiled=True)  20.9 us
    all_gather x1, blocking collectives, body(): pair = lax.all_gather(own, 'zh', axis=0, tiled=False)  16.3 us
    pallas_call x7, Pallas kernels, call(): pl.pallas_call(kernel, out_shape=outs, in_specs=[SMEM] * smem + [VMEM] *...  7.45 us
    ppermute x1, starting transfers between devices, body(): near = lax.ppermute(inward, SLAB, within + [(b, a) for a, b in within])  3.93 us
  transfers between devices with their start and end apart: 2, of which 0 were waited for; matrix products, arithmetic and copies ran while one was open for 0% of the time, Pallas kernels for 3%

profile of v7, /device:TPU:32, one launch (start us, length us, event | category | flops | bytes accessed | tf_op | source)
XLA Modules:
  0.0 96.4 jit_solution(13687431736817093468)
XLA Ops:
  0.6 0.0 copy-start
  0.6 0.0 copy-start.1
  0.7 2.0 %edges.1 = (f32[9,64,128]{2,1,0:T(8,128)S(1)}, f32[9,64,128]{2,1,0:T(8,128)S(1)}, f32[8,128]{1,0:T(8,128)S(1)}, s32[4]{0:T(128)S(1)}) custom-call(s32[32]{0:T(128)} %lengths.1, s32[32]{0:T(128)} %counts.1, s32[4,32]{1,0:T(4,128)} %bitcast.9, bf16[16,64,128]{2,1,0:T(8,128)(2,1)} %bitcast.5, f32[2,16,64,128]{3,2,1,0:T(8,128)} %fields.5), custom_call_target="tpu_custom_call" | custom-call | flops 1000000 | bytes 1905424 | tf_op jit(solution)/shard_map/edges/pallas_call | solution.py:331
  2.7 1.9 %collective-permute-start = (f32[9,64,128]{2,1,0:T(8,128)S(1)}, f32[9,64,128]{2,1,0:T(8,128)S(1)}, u32[]{:S(2)}, u32[]{:S(2)}) collective-permute-start(f32[9,64,128]{2,1,0:T(8,128)S(1)} %get-tuple-element.19), channel_id=1, source_target_pairs={{1,2},{3,4},{5,6},{7,8},{9,10},{11,12},{13,14},{2,1},{4,3},{6,5},{... | collective-permute-start | bytes 884744 | tf_op jit(solution)/shard_map/ppermute | solution.py:384
  4.6 3.9 %collective-permute-start.1 = (f32[9,64,128]{2,1,0:T(8,128)S(1)}, f32[9,64,128]{2,1,0:T(8,128)S(1)}, u32[]{:S(2)}, u32[]{:S(2)}) collective-permute-start(f32[9,64,128]{2,1,0:T(8,128)S(1)} %get-tuple-element.20), channel_id=1, source_target_pairs={{0,1},{2,3},{4,5},{6,7},{8,9},{10,11},{12,13},{14,15},{1,0},{3,2},... | collective-permute-start | bytes 884744 | tf_op jit(solution)/shard_map/ppermute | solution.py:385
  8.5 0.0 copy-done
  8.5 0.0 copy-done.1
  8.5 2.6 %inner.1 = (f32[2,16,64,128]{3,2,1,0:T(8,128)S(1)}, f32[4,4,64,128]{3,2,1,0:T(8,128)S(1)}, f32[16,2,64,128]{3,2,1,0:T(8,128)S(1)}, bf16[8,64,128]{2,1,0:T(8,128)...) custom-call(s32[4]{0:T(128)S(1)} %get-tuple-element.18.kinds, ...), custom_call_target="tpu_custom_call" | custom-call | flops 100000000 | bytes 5648400 | tf_op jit(solution)/shard_map/inner/pallas_call | solution.py:331
  11.2 0.0 collective-permute-done.outer
  11.2 0.0 collective-permute-done.1.near
  11.2 1.3 %outer.1 = (bf16[8,64,128]{2,1,0:T(8,128)(2,1)S(1)}, f32[8,2,64,128]{3,2,1,0:T(8,128)S(1)}, f32[16,2,128]{2,1,0:T(2,128)S(1)}) custom-call(s32[4]{0:T(128)S(1)} %get-tuple-element.18.kinds, f32[8,128]{1,0:T(8,128)S(1)} %get-tuple-element.17.params, f32[9,64,128]{2,1,0:T(8,128)S(1)} %collective-permute-done.outer, ...), custom_call_target="tpu_custom_call" | custom-call | flops 100000000 | bytes 4419600 | tf_op jit(solution)/shard_map/outer/pallas_call | solution.py:331
  12.5 20.9 %all_to_all.15.sums = f32[16,2,128]{2,1,0:T(2,128)S(1)} all-to-all(f32[16,2,128]{2,1,0:T(2,128)S(1)} %get-tuple-element.26), channel_id=1, replica_groups=mesh['zh'=2,'y'=4,'x'=4,'slab'=16] {'slab'}, dimensions={0} | all-to-all | bytes 32768 | tf_op jit(solution)/shard_map/all_to_all | solution.py:428
  33.4 0.2 weigh.1
  33.6 24.3 %all_to_all.16.arrived = f32[16,128,128]{2,1,0:T(8,128)S(1)} all-to-all(f32[16,128,128]{2,1,0:T(8,128)S(1)} %weigh.1), channel_id=1, replica_groups=mesh['zh'=2,'y'=4,'x'=4,'slab'=16] {'y','x'}, dimensions={0} | all-to-all | bytes 2097152 | tf_op jit(solution)/shard_map/all_to_all | solution.py:439
  57.9 0.1 reduce.1
  57.9 16.3 %all-gather = f32[256,128]{1,0:T(8,128)S(1)} all-gather(f32[128,128]{1,0:T(8,128)S(1)} %reduce.1), channel_id=2, replica_groups=mesh['zh'=2,'y'=4,'x'=4,'slab'=16] {'zh'}, dimensions={0}, use_global_device_ids=true | all-gather | bytes 196608 | tf_op jit(solution)/shard_map/all_gather | solution.py:441
  74.2 0.1 spread.1
  74.3 20.9 %all_to_all.17.blocks = f32[16,128,128]{2,1,0:T(8,128)S(1)} all-to-all(f32[16,128,128]{2,1,0:T(8,128)S(1)} %spread.1), channel_id=1, replica_groups=mesh['zh'=2,'y'=4,'x'=4,'slab'=16] {'y','x'}, dimensions={0} | all-to-all | bytes 2097152 | tf_op jit(solution)/shard_map/all_to_all | solution.py:445
  95.2 1.2 %update.1 = (f32[2,16,64,128]{3,2,1,0:T(8,128)}, bf16[16,64,128]{2,1,0:T(8,128)(2,1)}) custom-call(f32[16,128,128]{2,1,0:T(8,128)S(1)} %all_to_all.17.blocks, f32[2,16,64,128]{3,2,1,0:T(8,128)S(1)} %copy-done, bf16[8,64,128]{2,1,0:T(8,128)(2,1)S(1)} %get-tuple-element.28.middle, bf16[8,64,128]{2,1,0:T(8,128)(2,1)S(1)} %get-tuple-element.29.last), custom_call_target="tpu_custom_call" | custom-call | flops 1000000 | bytes 3670016 | tf_op jit(solution)/shard_map/update/pallas_call | solution.py:331
Async XLA Ops:
  0.6 7.9 %copy-start = (f32[2,16,64,128]{3,2,1,0:T(8,128)S(1)}, f32[2,16,64,128]{3,2,1,0:T(8,128)}, u32[]{:S(2)}) copy-start(f32[2,16,64,128]{3,2,1,0:T(8,128)} %fields.5) | copy-start | bytes 3145732
  0.6 7.9 %copy-start.1 = (bf16[1,16,64,128]{3,2,1,0:T(8,128)(2,1)S(1)}, bf16[1,16,64,128]{3,2,1,0:T(8,128)(2,1)}, u32[]{:S(2)}) copy-start(bf16[1,16,64,128]{3,2,1,0:T(8,128)(2,1)} %param.6) | copy-start | bytes 786436
  2.7 8.5 %collective-permute-start = (f32[9,64,128]{2,1,0:T(8,128)S(1)}, f32[9,64,128]{2,1,0:T(8,128)S(1)}, u32[]{:S(2)}, u32[]{:S(2)}) collective-permute-start(f32[9,64,128]{2,1,0:T(8,128)S(1)} %get-tuple-element.19), channel_id=1, source_target_pairs={{1,2},{3,4},{5,6},{7,8},{9,10},{11,12},{13,14},{2,1},{4,3},{6,5},{... | collective-permute-start | bytes 884744 | tf_op jit(solution)/shard_map/ppermute | solution.py:384
  4.6 6.6 %collective-permute-start.1 = (f32[9,64,128]{2,1,0:T(8,128)S(1)}, f32[9,64,128]{2,1,0:T(8,128)S(1)}, u32[]{:S(2)}, u32[]{:S(2)}) collective-permute-start(f32[9,64,128]{2,1,0:T(8,128)S(1)} %get-tuple-element.20), channel_id=1, source_target_pairs={{0,1},{2,3},{4,5},{6,7},{8,9},{10,11},{12,13},{14,15},{1,0},{3,2},... | collective-permute-start | bytes 884744 | tf_op jit(solution)/shard_map/ppermute | solution.py:385

commit v8 on v7

--- a/solution.py
+++ b/solution.py
@@ -9,7 +9,7 @@
 from jax.sharding import PartitionSpec as P
 
 CLS = ("zh", "y", "x")
-XY = ("y", "x")
+XY = ("x", "y")
 SLAB = "slab"
 
 flory_chi = 2.0

time: 96.7 us -> 96.3 us (level)
  no operation moved by 1% of the time
where the time goes in v8:
time: 96.3 us; the launch traced here: 96 us
  blocking collectives  81.9 us (85%)
  Pallas kernels  7.45 us (8%)
  starting transfers between devices  5.85 us (6%)
    all_to_all x1, blocking collectives, body(): arrived = lax.all_to_all(sent, XY, 0, 0, tiled=True)  24.2 us
    all_to_all x1, blocking collectives, body(): sums = lax.all_to_all(sums, SLAB, 0, 0, tiled=True)  20.9 us
    all_to_all x1, blocking collectives, body(): blocks = lax.all_to_all(blocks, XY, 0, 0, tiled=True)  20.8 us
    all_gather x1, blocking collectives, body(): pair = lax.all_gather(own, 'zh', axis=0, tiled=False)  16 us
    pallas_call x7, Pallas kernels, call(): pl.pallas_call(kernel, out_shape=outs, in_specs=[SMEM] * smem + [VMEM] *...  7.45 us
    ppermute x1, starting transfers between devices, body(): near = lax.ppermute(inward, SLAB, within + [(b, a) for a, b in within])  3.93 us
  transfers between devices with their start and end apart: 2, of which 0 were waited for; matrix products, arithmetic and copies ran while one was open for 0% of the time, Pallas kernels for 3%

profile of v8, /device:TPU:32, one launch (start us, length us, event | category | flops | bytes accessed | tf_op | source)
XLA Modules:
  0.0 96.0 jit_solution(16742327026313889896)
XLA Ops:
  0.6 0.0 copy-start
  0.6 0.0 copy-start.1
  0.7 2.0 %edges.1 = (f32[9,64,128]{2,1,0:T(8,128)S(1)}, f32[9,64,128]{2,1,0:T(8,128)S(1)}, f32[8,128]{1,0:T(8,128)S(1)}, s32[4]{0:T(128)S(1)}) custom-call(s32[32]{0:T(128)} %lengths.1, s32[32]{0:T(128)} %counts.1, s32[4,32]{1,0:T(4,128)} %bitcast.9, bf16[16,64,128]{2,1,0:T(8,128)(2,1)} %bitcast.5, f32[2,16,64,128]{3,2,1,0:T(8,128)} %fields.5), custom_call_target="tpu_custom_call" | custom-call | flops 1000000 | bytes 1905424 | tf_op jit(solution)/shard_map/edges/pallas_call | solution.py:331
  2.7 1.9 %collective-permute-start = (f32[9,64,128]{2,1,0:T(8,128)S(1)}, f32[9,64,128]{2,1,0:T(8,128)S(1)}, u32[]{:S(2)}, u32[]{:S(2)}) collective-permute-start(f32[9,64,128]{2,1,0:T(8,128)S(1)} %get-tuple-element.19), channel_id=1, source_target_pairs={{1,2},{3,4},{5,6},{7,8},{9,10},{11,12},{13,14},{2,1},{4,3},{6,5},{... | collective-permute-start | bytes 884744 | tf_op jit(solution)/shard_map/ppermute | solution.py:384
  4.6 3.9 %collective-permute-start.1 = (f32[9,64,128]{2,1,0:T(8,128)S(1)}, f32[9,64,128]{2,1,0:T(8,128)S(1)}, u32[]{:S(2)}, u32[]{:S(2)}) collective-permute-start(f32[9,64,128]{2,1,0:T(8,128)S(1)} %get-tuple-element.20), channel_id=1, source_target_pairs={{0,1},{2,3},{4,5},{6,7},{8,9},{10,11},{12,13},{14,15},{1,0},{3,2},... | collective-permute-start | bytes 884744 | tf_op jit(solution)/shard_map/ppermute | solution.py:385
  8.5 0.0 copy-done
  8.5 0.0 copy-done.1
  8.5 2.6 %inner.1 = (f32[2,16,64,128]{3,2,1,0:T(8,128)S(1)}, f32[4,4,64,128]{3,2,1,0:T(8,128)S(1)}, f32[16,2,64,128]{3,2,1,0:T(8,128)S(1)}, bf16[8,64,128]{2,1,0:T(8,128)...) custom-call(s32[4]{0:T(128)S(1)} %get-tuple-element.18.kinds, ...), custom_call_target="tpu_custom_call" | custom-call | flops 100000000 | bytes 5648400 | tf_op jit(solution)/shard_map/inner/pallas_call | solution.py:331
  11.2 0.0 collective-permute-done.outer
  11.2 0.0 collective-permute-done.1.near
  11.2 1.3 %outer.1 = (bf16[8,64,128]{2,1,0:T(8,128)(2,1)S(1)}, f32[8,2,64,128]{3,2,1,0:T(8,128)S(1)}, f32[16,2,128]{2,1,0:T(2,128)S(1)}) custom-call(s32[4]{0:T(128)S(1)} %get-tuple-element.18.kinds, f32[8,128]{1,0:T(8,128)S(1)} %get-tuple-element.17.params, f32[9,64,128]{2,1,0:T(8,128)S(1)} %collective-permute-done.outer, ...), custom_call_target="tpu_custom_call" | custom-call | flops 100000000 | bytes 4419600 | tf_op jit(solution)/shard_map/outer/pallas_call | solution.py:331
  12.5 20.9 %all_to_all.15.sums = f32[16,2,128]{2,1,0:T(2,128)S(1)} all-to-all(f32[16,2,128]{2,1,0:T(2,128)S(1)} %get-tuple-element.26), channel_id=1, replica_groups=mesh['zh'=2,'y'=4,'x'=4,'slab'=16] {'slab'}, dimensions={0} | all-to-all | bytes 32768 | tf_op jit(solution)/shard_map/all_to_all | solution.py:428
  33.4 0.2 weigh.1
  33.6 24.2 %all_to_all.16.arrived = f32[16,128,128]{2,1,0:T(8,128)S(1)} all-to-all(f32[16,128,128]{2,1,0:T(8,128)S(1)} %weigh.1), channel_id=1, replica_groups=mesh['zh'=2,'y'=4,'x'=4,'slab'=16] {'x','y'}, dimensions={0} | all-to-all | bytes 2097152 | tf_op jit(solution)/shard_map/all_to_all | solution.py:439
  57.8 0.1 reduce.1
  57.9 16.0 %all-gather = f32[256,128]{1,0:T(8,128)S(1)} all-gather(f32[128,128]{1,0:T(8,128)S(1)} %reduce.1), channel_id=2, replica_groups=mesh['zh'=2,'y'=4,'x'=4,'slab'=16] {'zh'}, dimensions={0}, use_global_device_ids=true | all-gather | bytes 196608 | tf_op jit(solution)/shard_map/all_gather | solution.py:441
  73.9 0.1 spread.1
  74.0 20.8 %all_to_all.17.blocks = f32[16,128,128]{2,1,0:T(8,128)S(1)} all-to-all(f32[16,128,128]{2,1,0:T(8,128)S(1)} %spread.1), channel_id=1, replica_groups=mesh['zh'=2,'y'=4,'x'=4,'slab'=16] {'x','y'}, dimensions={0} | all-to-all | bytes 2097152 | tf_op jit(solution)/shard_map/all_to_all | solution.py:445
  94.8 1.2 %update.1 = (f32[2,16,64,128]{3,2,1,0:T(8,128)}, bf16[16,64,128]{2,1,0:T(8,128)(2,1)}) custom-call(f32[16,128,128]{2,1,0:T(8,128)S(1)} %all_to_all.17.blocks, f32[2,16,64,128]{3,2,1,0:T(8,128)S(1)} %copy-done, bf16[8,64,128]{2,1,0:T(8,128)(2,1)S(1)} %get-tuple-element.28.middle, bf16[8,64,128]{2,1,0:T(8,128)(2,1)S(1)} %get-tuple-element.29.last), custom_call_target="tpu_custom_call" | custom-call | flops 1000000 | bytes 3670016 | tf_op jit(solution)/shard_map/update/pallas_call | solution.py:331
Async XLA Ops:
  0.6 7.9 %copy-start = (f32[2,16,64,128]{3,2,1,0:T(8,128)S(1)}, f32[2,16,64,128]{3,2,1,0:T(8,128)}, u32[]{:S(2)}) copy-start(f32[2,16,64,128]{3,2,1,0:T(8,128)} %fields.5) | copy-start | bytes 3145732
  0.6 7.9 %copy-start.1 = (bf16[1,16,64,128]{3,2,1,0:T(8,128)(2,1)S(1)}, bf16[1,16,64,128]{3,2,1,0:T(8,128)(2,1)}, u32[]{:S(2)}) copy-start(bf16[1,16,64,128]{3,2,1,0:T(8,128)(2,1)} %param.6) | copy-start | bytes 786436
  2.7 8.5 %collective-permute-start = (f32[9,64,128]{2,1,0:T(8,128)S(1)}, f32[9,64,128]{2,1,0:T(8,128)S(1)}, u32[]{:S(2)}, u32[]{:S(2)}) collective-permute-start(f32[9,64,128]{2,1,0:T(8,128)S(1)} %get-tuple-element.19), channel_id=1, source_target_pairs={{1,2},{3,4},{5,6},{7,8},{9,10},{11,12},{13,14},{2,1},{4,3},{6,5},{... | collective-permute-start | bytes 884744 | tf_op jit(solution)/shard_map/ppermute | solution.py:384
  4.6 6.6 %collective-permute-start.1 = (f32[9,64,128]{2,1,0:T(8,128)S(1)}, f32[9,64,128]{2,1,0:T(8,128)S(1)}, u32[]{:S(2)}, u32[]{:S(2)}) collective-permute-start(f32[9,64,128]{2,1,0:T(8,128)S(1)} %get-tuple-element.20), channel_id=1, source_target_pairs={{0,1},{2,3},{4,5},{6,7},{8,9},{10,11},{12,13},{14,15},{1,0},{3,2},... | collective-permute-start | bytes 884744 | tf_op jit(solution)/shard_map/ppermute | solution.py:385

commit v9 on v8

--- a/solution.py
+++ b/solution.py
@@ -82,16 +82,10 @@
     planes = q.shape[0]
     depth = types.shape[0]
     cls = own_class()
-    messages = (outward, inward)
     copies = [(lengths, own_lengths), (counts, own_counts), (types, own_types)]
-    for m, upper in enumerate(sides()):
-        start, turn = upper * (planes - depth) + (1 - upper) * (depth - 1), 2 * upper - 1
-        for r in range(depth):
-            at = start + turn * r
-            copies.append((q.at[at], ends.at[m, r]))
-            for t in range(2):
-                to = raw.at[m, 2 * r + t] if r < 2 else messages[m].at[depth + 1 + 2 * (r - 2) + t]
-                copies.append((fields.at[t, at], to))
+    for side, start in enumerate((0, planes - depth)):
+        copies.append((q.at[pl.ds(start, depth)], ends.at[side]))
+        copies.append((fields.at[:, pl.ds(start, depth)], raw.at[side]))
     copies = [pltpu.make_async_copy(a, b, sems.at[i]) for i, (a, b) in enumerate(copies)]
     for copy in copies:
         copy.start()
@@ -111,11 +105,16 @@
     scale = -0.5 * size
     for copy in copies[3:]:
         copy.wait()
-    for m, message in enumerate(messages):
+    for message, upper in zip((outward, inward), sides()):
         for r in range(depth):
-            chosen = raw[m, 2 * r + first] if r < 2 else message[depth + 1 + 2 * (r - 2) + first]
-            message[r] = jnp.exp(scale * chosen) * ends[m, r].astype(jnp.float32)
-        message[depth] = jnp.exp(scale * (raw[m, 2 + first] + raw[m, 2 + second]))
+            at = upper * r + (1 - upper) * (depth - 1 - r)
+            chosen = raw[upper, first, at]
+            message[r] = jnp.exp(scale * chosen) * ends[upper, at].astype(jnp.float32)
+            if r == 1:
+                message[depth] = jnp.exp(scale * (chosen + raw[upper, second, at]))
+            elif r > 1:
+                for t in range(2):
+                    message[depth + 1 + 2 * (r - 2) + t] = raw[upper, t, at]
 
 
 def inner_kernel(
@@ -365,11 +364,11 @@
         [message, message, f32(8, ny), jax.ShapeDtypeStruct((depth,), jnp.int32)],
         [
             pltpu.VMEM((2, depth, nx, ny), jnp.bfloat16),
-            pltpu.VMEM((2, 4, nx, ny), jnp.float32),
+            pltpu.VMEM((2, 2, depth, nx, ny), jnp.float32),
             pltpu.SMEM((classes,), jnp.int32),
             pltpu.SMEM((classes,), jnp.int32),
             pltpu.SMEM((depth, classes), jnp.int32),
-            pltpu.SemaphoreType.DMA((6 * depth + 3,)),
+            pltpu.SemaphoreType.DMA((7,)),
         ],
         tuple(map(in_hbm, (lengths, counts, types, q, fields))),
         0,

time: 96.3 us -> 96.1 us (level)
  no operation moved by 1% of the time
where the time goes in v9:
time: 96.1 us; the launch traced here: 95.8 us
  blocking collectives  81.9 us (85%)
  Pallas kernels  7.31 us (8%)
  starting transfers between devices  5.85 us (6%)
    all_to_all x1, blocking collectives, body(): arrived = lax.all_to_all(sent, XY, 0, 0, tiled=True)  24.2 us
    all_to_all x1, blocking collectives, body(): sums = lax.all_to_all(sums, SLAB, 0, 0, tiled=True)  20.9 us
    all_to_all x1, blocking collectives, body(): blocks = lax.all_to_all(blocks, XY, 0, 0, tiled=True)  20.8 us
    all_gather x1, blocking collectives, body(): pair = lax.all_gather(own, 'zh', axis=0, tiled=False)  16 us
    pallas_call x7, Pallas kernels, call(): pl.pallas_call(kernel, out_shape=outs, in_specs=[SMEM] * smem + [VMEM] *...  7.31 us
    ppermute x1, starting transfers between devices, body(): near = lax.ppermute(inward, SLAB, within + [(b, a) for a, b in within])  3.93 us
  transfers between devices with their start and end apart: 2, of which 0 were waited for; matrix products, arithmetic and copies ran while one was open for 0% of the time, Pallas kernels for 3%

profile of v9, /device:TPU:32, one launch (start us, length us, event | category | flops | bytes accessed | tf_op | source)
XLA Modules:
  0.0 95.8 jit_solution(10776908555185917366)
XLA Ops:
  0.6 0.0 copy-start
  0.6 0.0 copy-start.1
  0.7 1.9 %edges.1 = (f32[9,64,128]{2,1,0:T(8,128)S(1)}, f32[9,64,128]{2,1,0:T(8,128)S(1)}, f32[8,128]{1,0:T(8,128)S(1)}, s32[4]{0:T(128)S(1)}) custom-call(s32[32]{0:T(128)} %lengths.1, s32[32]{0:T(128)} %counts.1, s32[4,32]{1,0:T(4,128)} %bitcast.9, bf16[16,64,128]{2,1,0:T(8,128)(2,1)} %bitcast.5, f32[2,16,64,128]{3,2,1,0:T(8,128)} %fields.5), custom_call_target="tpu_custom_call" | custom-call | flops 1000000 | bytes 1905424 | tf_op jit(solution)/shard_map/edges/pallas_call | solution.py:330
  2.5 1.9 %collective-permute-start = (f32[9,64,128]{2,1,0:T(8,128)S(1)}, f32[9,64,128]{2,1,0:T(8,128)S(1)}, u32[]{:S(2)}, u32[]{:S(2)}) collective-permute-start(f32[9,64,128]{2,1,0:T(8,128)S(1)} %get-tuple-element.19), channel_id=1, source_target_pairs={{1,2},{3,4},{5,6},{7,8},{9,10},{11,12},{13,14},{2,1},{4,3},{6,5},{... | collective-permute-start | bytes 884744 | tf_op jit(solution)/shard_map/ppermute | solution.py:383
  4.4 3.9 %collective-permute-start.1 = (f32[9,64,128]{2,1,0:T(8,128)S(1)}, f32[9,64,128]{2,1,0:T(8,128)S(1)}, u32[]{:S(2)}, u32[]{:S(2)}) collective-permute-start(f32[9,64,128]{2,1,0:T(8,128)S(1)} %get-tuple-element.20), channel_id=1, source_target_pairs={{0,1},{2,3},{4,5},{6,7},{8,9},{10,11},{12,13},{14,15},{1,0},{3,2},... | collective-permute-start | bytes 884744 | tf_op jit(solution)/shard_map/ppermute | solution.py:384
  8.4 0.0 copy-done
  8.4 0.0 copy-done.1
  8.4 2.6 %inner.1 = (f32[2,16,64,128]{3,2,1,0:T(8,128)S(1)}, f32[4,4,64,128]{3,2,1,0:T(8,128)S(1)}, f32[16,2,64,128]{3,2,1,0:T(8,128)S(1)}, bf16[8,64,128]{2,1,0:T(8,128)...) custom-call(s32[4]{0:T(128)S(1)} %get-tuple-element.18.kinds, ...), custom_call_target="tpu_custom_call" | custom-call | flops 100000000 | bytes 5648400 | tf_op jit(solution)/shard_map/inner/pallas_call | solution.py:330
  11.0 0.0 collective-permute-done.outer
  11.0 0.0 collective-permute-done.1.near
  11.0 1.3 %outer.1 = (bf16[8,64,128]{2,1,0:T(8,128)(2,1)S(1)}, f32[8,2,64,128]{3,2,1,0:T(8,128)S(1)}, f32[16,2,128]{2,1,0:T(2,128)S(1)}) custom-call(s32[4]{0:T(128)S(1)} %get-tuple-element.18.kinds, f32[8,128]{1,0:T(8,128)S(1)} %get-tuple-element.17.params, f32[9,64,128]{2,1,0:T(8,128)S(1)} %collective-permute-done.outer, ...), custom_call_target="tpu_custom_call" | custom-call | flops 100000000 | bytes 4419600 | tf_op jit(solution)/shard_map/outer/pallas_call | solution.py:330
  12.3 20.9 %all_to_all.15.sums = f32[16,2,128]{2,1,0:T(2,128)S(1)} all-to-all(f32[16,2,128]{2,1,0:T(2,128)S(1)} %get-tuple-element.26), channel_id=1, replica_groups=mesh['zh'=2,'y'=4,'x'=4,'slab'=16] {'slab'}, dimensions={0} | all-to-all | bytes 32768 | tf_op jit(solution)/shard_map/all_to_all | solution.py:427
  33.2 0.2 weigh.1
  33.4 24.2 %all_to_all.16.arrived = f32[16,128,128]{2,1,0:T(8,128)S(1)} all-to-all(f32[16,128,128]{2,1,0:T(8,128)S(1)} %weigh.1), channel_id=1, replica_groups=mesh['zh'=2,'y'=4,'x'=4,'slab'=16] {'x','y'}, dimensions={0} | all-to-all | bytes 2097152 | tf_op jit(solution)/shard_map/all_to_all | solution.py:438
  57.7 0.1 reduce.1
  57.7 16.0 %all-gather = f32[256,128]{1,0:T(8,128)S(1)} all-gather(f32[128,128]{1,0:T(8,128)S(1)} %reduce.1), channel_id=2, replica_groups=mesh['zh'=2,'y'=4,'x'=4,'slab'=16] {'zh'}, dimensions={0}, use_global_device_ids=true | all-gather | bytes 196608 | tf_op jit(solution)/shard_map/all_gather | solution.py:440
  73.8 0.1 spread.1
  73.9 20.8 %all_to_all.17.blocks = f32[16,128,128]{2,1,0:T(8,128)S(1)} all-to-all(f32[16,128,128]{2,1,0:T(8,128)S(1)} %spread.1), channel_id=1, replica_groups=mesh['zh'=2,'y'=4,'x'=4,'slab'=16] {'x','y'}, dimensions={0} | all-to-all | bytes 2097152 | tf_op jit(solution)/shard_map/all_to_all | solution.py:444
  94.7 1.2 %update.1 = (f32[2,16,64,128]{3,2,1,0:T(8,128)}, bf16[16,64,128]{2,1,0:T(8,128)(2,1)}) custom-call(f32[16,128,128]{2,1,0:T(8,128)S(1)} %all_to_all.17.blocks, f32[2,16,64,128]{3,2,1,0:T(8,128)S(1)} %copy-done, bf16[8,64,128]{2,1,0:T(8,128)(2,1)S(1)} %get-tuple-element.28.middle, bf16[8,64,128]{2,1,0:T(8,128)(2,1)S(1)} %get-tuple-element.29.last), custom_call_target="tpu_custom_call" | custom-call | flops 1000000 | bytes 3670016 | tf_op jit(solution)/shard_map/update/pallas_call | solution.py:330
Async XLA Ops:
  0.6 7.8 %copy-start = (f32[2,16,64,128]{3,2,1,0:T(8,128)S(1)}, f32[2,16,64,128]{3,2,1,0:T(8,128)}, u32[]{:S(2)}) copy-start(f32[2,16,64,128]{3,2,1,0:T(8,128)} %fields.5) | copy-start | bytes 3145732
  0.6 7.8 %copy-start.1 = (bf16[1,16,64,128]{3,2,1,0:T(8,128)(2,1)S(1)}, bf16[1,16,64,128]{3,2,1,0:T(8,128)(2,1)}, u32[]{:S(2)}) copy-start(bf16[1,16,64,128]{3,2,1,0:T(8,128)(2,1)} %param.6) | copy-start | bytes 786436
  2.5 8.5 %collective-permute-start = (f32[9,64,128]{2,1,0:T(8,128)S(1)}, f32[9,64,128]{2,1,0:T(8,128)S(1)}, u32[]{:S(2)}, u32[]{:S(2)}) collective-permute-start(f32[9,64,128]{2,1,0:T(8,128)S(1)} %get-tuple-element.19), channel_id=1, source_target_pairs={{1,2},{3,4},{5,6},{7,8},{9,10},{11,12},{13,14},{2,1},{4,3},{6,5},{... | collective-permute-start | bytes 884744 | tf_op jit(solution)/shard_map/ppermute | solution.py:383
  4.4 6.6 %collective-permute-start.1 = (f32[9,64,128]{2,1,0:T(8,128)S(1)}, f32[9,64,128]{2,1,0:T(8,128)S(1)}, u32[]{:S(2)}, u32[]{:S(2)}) collective-permute-start(f32[9,64,128]{2,1,0:T(8,128)S(1)} %get-tuple-element.20), channel_id=1, source_target_pairs={{0,1},{2,3},{4,5},{6,7},{8,9},{10,11},{12,13},{14,15},{1,0},{3,2},... | collective-permute-start | bytes 884744 | tf_op jit(solution)/shard_map/ppermute | solution.py:384
